TPU v7x, 32 devices: a whole 2x2x4 slice. The times are simulated.
32 devices in a mesh: tm: 2 (over x), gx: 4 (over y, core), gy: 4 (over z).
Axes of the slice: x: 2, y: 2, z: 4, core: 2. Of those that a mesh axis runs over, the one named last changes fastest.
Arguments:
- trajectory: float32 [4, 3, 128, 1024], P('tm', None, 'gy', 'gx'), may hold values from -3 to 3
- initial: float32 [3, 128, 1024], P(None, 'gy', 'gx'), may hold values from -3 to 3
Outputs:
- updated: float32 [4, 3, 128, 1024], P('tm', None, 'gy', 'gx')
- residual: float32 [4, 3, 128, 1024], P('tm', None, 'gy', 'gx')
All inputs are finite; a program needn't handle non-finite values.
Results may differ from a plain program's by a relative error of at most 0.00023.
Values sent between devices are 32-bit elements; how exact they have to be, the bound alone decides.
No kernel may reach another device: no remote copies, remote signals or barrier semaphores. Data moves between devices by JAX's collectives and lax.ppermute only.
A program may use at most 64 MiB of HBM per device.

v0:
```python
import cmath
import functools
import math
import operator

import jax
import jax.numpy as jnp
from jax import lax
from jax.experimental import pallas as pl
from jax.experimental.pallas import tpu as pltpu
from jax.sharding import PartitionSpec as P


CHEB = 6
COURANT = 1.5
CORIOLIS_MEAN = 0.3
CORIOLIS_SLOPE = 0.4
CIRCULANT = 0.1
SPECTRUM_EDGE = 5.0
REACH = CHEB + 1
HALO = 8
LANES = 128
VMEM_KEPT = 2**20
SUBLANES = 8


def polynomials(total):
    factor = math.exp(math.log(CIRCULANT) / total)
    table = [[0.0] * (CHEB + 1) for _ in range(total)]
    for k in range(total):
        angle = 2.0 * math.pi * k / total
        shift = complex(1.0 - factor * math.cos(angle), factor * math.sin(angle))
        edge = 1j * SPECTRUM_EDGE
        sigma = shift / edge
        rho_old = 1.0 / sigma
        update = [1.0 / shift] + [0.0] * CHEB
        solved = list(update)
        for _ in range(CHEB):
            misfit = [-shift * solved[j] - (solved[j - 1] if j else -1.0) for j in range(CHEB + 1)]
            rho_new = 1.0 / (2.0 * sigma - rho_old)
            update = [rho_new * rho_old * a + 2.0 * rho_new / edge * b for a, b in zip(update, misfit)]
            solved = [a + b for a, b in zip(solved, update)]
            rho_old = rho_new
        for lag in range(total):
            turn = cmath.exp(1j * angle * lag) / total
            for j in range(CHEB + 1):
                table[lag][j] += (turn * solved[j]).real * COURANT**j
    return table


def pair_up(axis, odd):
    count = lax.axis_size(axis)
    first = range(1 if odd else 0, count, 2)
    return [pair for i in first for pair in ((i, (i + 1) % count), ((i + 1) % count, i))]


def with_steps(axis, pairs, by):
    times, count = lax.axis_size("tm"), lax.axis_size(axis)
    return [(t * count + a, (t + by) % times * count + b) for t in range(times) for a, b in pairs]


def rotated(tiles, by):
    lane = lax.broadcasted_iota(jnp.int32, (SUBLANES, LANES), 1)
    turned = [pltpu.roll(tile, by % LANES, 1) for tile in tiles]
    if len(tiles) == 1:
        return turned
    edge = lane == (0 if by > 0 else LANES - 1)
    return [jnp.where(edge, turned[(w - by) % len(tiles)], turned[w]) for w in range(len(tiles))]


def dlon(tiles):
    return [east - west for east, west in zip(rotated(tiles, -1), rotated(tiles, 1))]


def around(load, q, tiles):
    north = load(q - 1) if q else [pltpu.roll(tile, 1, 0) for tile in load(tiles - 1)]
    south = load(q + 1) if q < tiles - 1 else [pltpu.roll(tile, SUBLANES - 1, 0) for tile in load(0)]
    return north, south


def dlat(load, q, tiles):
    north, south = around(load, q, tiles)
    return [s - n for s, n in zip(south, north)]


def dealt(ref, f, q):
    tiles = ref.shape[-2] // SUBLANES
    return [ref[f, w, pl.ds(q, SUBLANES, stride=tiles), :] for w in range(ref.shape[1])]


def gather_columns(tiles, width):
    lane = lax.broadcasted_iota(jnp.int32, (SUBLANES, LANES), 1)
    packed = jnp.zeros((SUBLANES, LANES), jnp.float32)
    half = LANES // 2
    for f, tile in enumerate(tiles):
        head = pltpu.roll(tile[:, :LANES], half + REACH * f, 1)
        tail = pltpu.roll(tile[:, width - LANES :], REACH * (f + 1), 1)
        at = lane - REACH * f
        packed = jnp.where((at >= 0) & (at < REACH), tail, packed)
        packed = jnp.where((at >= half) & (at < half + REACH), head, packed)
    return packed


def split_kernel(fields, traj, init, own, zs_even, zs_odd, packs):
    rows_lat, width = traj.shape[-2:]
    gy_even = lax.axis_index("gy") % 2 == 0
    for f in range(fields + 3):
        field = traj[f // 3, f % 3] if f < fields else init[f - fields]
        own[f] = field
        north, south = (field[:HALO], field[rows_lat - HALO :])
        zs_even[f] = jnp.where(gy_even, south, north)
        zs_odd[f] = jnp.where(gy_even, north, south)
    for rows in range(rows_lat // SUBLANES):
        at = pl.ds(rows * SUBLANES, SUBLANES)
        packs[at, :] = gather_columns([own.at[f, at] for f in range(fields + 3)], width)


def pack_kernel(fields, packs, zr_even, zr_odd, xs, ys):
    width = zr_even.shape[-1]
    gy_even = lax.axis_index("gy") % 2 == 0
    rows_lat = packs.shape[0]
    xs[:fields] = zr_even[:fields]
    xs[fields:] = zr_odd[:fields]
    even = gather_columns([zr_even.at[f] for f in range(fields + 3)], width)
    odd = gather_columns([zr_odd.at[f] for f in range(fields + 3)], width)
    ys[:HALO, :] = jnp.where(gy_even, odd, even)
    ys[HALO : HALO + rows_lat, :] = packs[...]
    ys[HALO + rows_lat :, :] = jnp.where(gy_even, even, odd)


def place(ext, base, own, even, odd):
    rows_lat, width = own[0].shape
    gy_even = lax.axis_index("gy") % 2 == 0
    for f, field in enumerate(own):
        for w in range(width // LANES):
            lanes = pl.ds(w * LANES, LANES)
            ext[base + f, w, pl.ds(HALO, rows_lat), :] = field[:, lanes]
            ext[base + f, w, pl.ds(0, HALO), :] = jnp.where(gy_even, odd[f, :, lanes], even[f, :, lanes])
            ext[base + f, w, pl.ds(rows_lat + HALO, HALO), :] = jnp.where(gy_even, even[f, :, lanes], odd[f, :, lanes])


def within(first, count, by=0):
    lane = lax.broadcasted_iota(jnp.int32, (SUBLANES, LANES), 1)
    return (lane - first - by) % LANES < count


def place_strips(strips, ext, count):
    tiles = ext.shape[1]
    for rows in range(ext.shape[2] // SUBLANES):
        rows = pl.ds(rows * SUBLANES, SUBLANES)
        for f in range(count):
            head = pltpu.roll(ext[f, 0, rows, :], LANES // 2 + REACH, 1)
            strips[f, rows, :] = jnp.where(within(LANES // 2 + REACH, 2 * REACH), head, ext[f, tiles - 1, rows, :])


def place_rim(rim, strips, at, count, slot, pack_even, pack_odd):
    half = LANES // 2
    lane = lax.broadcasted_iota(jnp.int32, (SUBLANES, LANES), 1)
    gx_even = lax.axis_index("gx") % 2 == 0
    from_odd = (lane < half) == gx_even
    outside = within(0, REACH) | within(half, REACH)
    for rows in range(strips.shape[1] // SUBLANES):
        rows = pl.ds(rows * SUBLANES, SUBLANES)
        both = jnp.where(from_odd, pack_odd[rows, :], pack_even[rows, :])
        for f in range(count):
            value = pltpu.roll(both, half - REACH * (slot + f), 1)
            rim[at + f, 0, rows, :] = jnp.where(outside, value, strips[at + f, rows, :])


def coriolis(q, rows_lat):
    gy = lax.axis_index("gy")
    nlat = rows_lat * lax.axis_size("gy")
    tiles = (rows_lat + 2 * HALO) // SUBLANES
    row = lax.broadcasted_iota(jnp.int32, (SUBLANES, LANES), 0) * tiles + (q - HALO) + gy * rows_lat
    row = jnp.where(row < 0, row + nlat, jnp.where(row >= nlat, row - nlat, row))
    return CORIOLIS_MEAN + CORIOLIS_SLOPE * ((row.astype(jnp.float32) + 0.5) / nlat - 0.5)


def tendency(load, q, tiles, rotation):
    h, u, v = (load(c, q) for c in range(3))

    def product(at):
        return [b + a * b for a, b in zip(load(0, at), load(2, at))]

    flow = dlon([b + a * b for a, b in zip(h, u)])
    east = [dlon(field) for field in (h, u, v)]
    north = [dlat(functools.partial(load, c), q, tiles) for c in range(3)]
    drift = dlat(product, q, tiles)
    out = ([], [], [])
    for w in range(len(h)):
        out[0].append(h[w] + COURANT * (flow[w] + drift[w]))
        out[1].append(u[w] - rotation * v[w] + COURANT * (east[0][w] + u[w] * east[1][w] + v[w] * north[1][w]))
        out[2].append(v[w] + rotation * u[w] + COURANT * (north[0][w] + u[w] * east[2][w] + v[w] * north[2][w]))
    return out


def horner(rates, weights, state, turn, write):
    outputs, (tiles, across) = range(len(weights)), rates.shape[1:3]

    def blend(n, j, c, q):
        terms = lambda t: (w[j] * rates[3 * i + c, q, t] for i, w in enumerate(weights[n]))
        return [functools.reduce(operator.add, terms(t)) for t in range(across)]

    for q in range(tiles):
        for n in outputs:
            for c in range(3):
                for t, value in enumerate(blend(n, CHEB, c, q)):
                    state[0, n, c, q, t] = value
    for j in range(CHEB - 1, -1, -1):
        now, later = ((CHEB - 1 - j) % 2, (CHEB - j) % 2)
        for q in range(tiles):
            for n in outputs:
                load = lambda c, at, n=n: [state[now, n, c, at, t] for t in range(across)]
                h, u, v = (load(c, q) for c in range(3))
                east_h, east_u = (dlon(h), dlon(u))
                north_h, north_v = (dlat(functools.partial(load, c), q, tiles) for c in (0, 2))
                add = [blend(n, j, c, q) for c in range(3)]
                new = (
                    [add[0][t] + (east_u[t] + north_v[t]) for t in range(across)],
                    [add[1][t] + (east_h[t] - turn[q] * v[t]) for t in range(across)],
                    [add[2][t] + (north_h[t] + turn[q] * u[t]) for t in range(across)],
                )
                for c in range(3):
                    if j:
                        for t in range(across):
                            state[later, n, c, q, t] = new[c][t]
                    else:
                        write(n, c, q, new[c])


def weights_of(lags, lag):
    return [w * CIRCULANT ** (-lag / len(lags)) for w in lags[lag % len(lags)]]


def put(scratch, f, q, values):
    tiles = scratch.shape[-2] // SUBLANES
    for w, value in enumerate(values):
        scratch[f, w, pl.ds(q, SUBLANES, stride=tiles), :] = value


def block_of(scratch, f, rows_lat):
    return jnp.concatenate([scratch[f, w, HALO : HALO + rows_lat] for w in range(scratch.shape[1])], axis=1)


def residuals(times, steps, ext, rates, rotation, write):
    fields, first = 3 * steps, 3 * steps * times
    tiles = rates.shape[1]
    me = lax.axis_index("tm")
    for d in range(times):
        scale = jnp.where(me < d, jnp.float32(CIRCULANT), jnp.float32(1.0))
        for l in range(steps):
            at = d * fields + 3 * l
            before = (at - 3) if l else ((d + 1) % times * fields + fields - 3)
            for q in range(tiles):
                out = tendency(lambda c, row: dealt(ext, at + c, row), q, tiles, rotation[q])
                for c in range(3):
                    prior = dealt(ext, before + c, q)
                    if l == 0:
                        prior = [jnp.where(me == d, a, b) for a, b in zip(dealt(ext, first + c, q), prior)]
                    values = [a - b for a, b in zip(out[c], prior)]
                    if d == 0:
                        write(l, c, q, values)
                    for t, value in enumerate(values):
                        rates[at + c, q, t] = scale * value if d else value


def weights_for(times, steps, lags):
    return [
        [weights_of(lags, d * steps + n - m) for d in range(times) for m in range(steps)] for n in range(steps)
    ]


def block_kernel(times, steps, lags, own, zr_even, zr_odd, *refs):
    fields = 3 * steps
    others = refs[: 2 * (times - 1)]
    strips, part, residual, ext, rates, state, scratch = refs[2 * (times - 1) :]
    rows_lat = own.shape[-2]
    place(ext, 0, [own.at[f] for f in range(fields)], zr_even.at[:fields], zr_odd.at[:fields])
    for d in range(1, times):
        raw, xr = others[2 * (d - 1) : 2 * d]
        blocks = [raw.at[f // 3, f % 3] for f in range(fields)]
        place(ext, d * fields, blocks, xr.at[:fields], xr.at[fields:])
    place(ext, times * fields, [own.at[fields + c] for c in range(3)], zr_even.at[fields:], zr_odd.at[fields:])
    rotation = [coriolis(q, rows_lat) for q in range(rates.shape[1])]
    residuals(times, steps, ext, rates, rotation, lambda l, c, q, values: put(scratch, 3 * l + c, q, values))
    for l in range(steps):
        for c in range(3):
            residual[l, c] = block_of(scratch, 3 * l + c, rows_lat)
    place_strips(strips, ext, times * fields + 3)
    turn = [r * (1.0 / COURANT) for r in rotation]
    weights = weights_for(times, steps, lags)
    horner(rates, weights, state, turn, lambda n, c, q, values: put(scratch, fields + 3 * n + c, q, values))
    for n in range(steps):
        for c in range(3):
            part[n, c] = block_of(scratch, fields + 3 * n + c, rows_lat)


APART = 4 * REACH


def rim_kernel(times, steps, lags, own, strips, part, part_residual, yr_even, yr_odd, *refs):
    fields, half = 3 * steps, LANES // 2
    packs = refs[: 2 * (times - 1)]
    updated, residual, rim, rates, state, scratch = refs[2 * (times - 1) :]
    rows_lat, width = own.shape[-2:]
    tiles = rates.shape[1]
    place_rim(rim, strips, 0, fields, 0, yr_even, yr_odd)
    place_rim(rim, strips, times * fields, 3, fields, yr_even, yr_odd)
    for d in range(1, times):
        place_rim(rim, strips, d * fields, fields, 0, *packs[2 * (d - 1) : 2 * d])
    rotation = [coriolis(q, rows_lat) for q in range(tiles)]
    residuals(times, steps, rim, rates, rotation, lambda l, c, q, values: put(scratch, 3 * l + c, q, values))
    lane = lax.broadcasted_iota(jnp.int32, (rows_lat, LANES), 1)

    def merged(value, strip, by):
        tail = pltpu.roll(strip, LANES - by, 1) if by else strip
        head = pltpu.roll(strip, half - REACH - by, 1)
        value = [value[:, w * LANES : (w + 1) * LANES] for w in range(width // LANES)]
        value[0] = jnp.where(lane < REACH, head, value[0])
        value[-1] = jnp.where(lane >= LANES - REACH, tail, value[-1])
        return jnp.concatenate(value, axis=1)

    for l in range(steps):
        for c in range(3):
            residual[l, c] = merged(part_residual[l, c], block_of(scratch, 3 * l + c, rows_lat), 0)

    second = within(LANES - 2 * REACH, 3 * REACH, APART) | within(half, 3 * REACH, APART)
    for f in range(times * fields):
        for q in range(tiles):
            rates[f, q, 0] = jnp.where(second, pltpu.roll(rates[f, q, 0], APART, 1), rates[f, q, 0])
    turn = [r * (1.0 / COURANT) for r in rotation]
    plain = weights_for(times, steps, lags)
    for n in range(0, steps, 2):
        pair = [
            [[jnp.where(second, b, a) for a, b in zip(*both)] for both in zip(plain[n], plain[min(n + 1, steps - 1)])]
        ]
        horner(rates, pair, state, turn, lambda _, c, q, values: put(scratch, c, q, values))
        for c in range(3):
            strip = block_of(scratch, c, rows_lat)
            for m in range(n, min(n + 2, steps)):
                updated[m, c] = own[3 * m + c] - merged(part[m, c], strip, (m - n) * APART)


def step(trajectory, initial):
    steps, _, rows_lat, width = trajectory.shape
    times = lax.axis_size("tm")
    fields = 3 * steps
    lags = polynomials(times * steps)

    def vmem(*shape):
        return pltpu.VMEM(shape, jnp.float32)

    rows, across = (rows_lat + 2 * HALO, width // LANES)
    known = times * fields

    def hbm(*shape):
        return jax.ShapeDtypeStruct(shape, jnp.float32)

    fits = 4 * known * rows * width <= VMEM_KEPT
    near = vmem if fits else hbm

    def kept(*arrays):
        return [pltpu.with_memory_space_constraint(array, pltpu.VMEM) if fits else array for array in arrays]

    own, zs_even, zs_odd, packs = pl.pallas_call(
        functools.partial(split_kernel, fields),
        out_shape=(
            near(fields + 3, rows_lat, width),
            near(fields + 3, HALO, width),
            near(fields + 3, HALO, width),
            near(rows_lat, LANES),
        ),
        name="split_edges",
    )(trajectory, initial)
    zr_odd = lax.ppermute(zs_odd, "gy", pair_up("gy", True))
    zr_even = lax.ppermute(zs_even, "gy", pair_up("gy", False))
    shifts = [[(t, (t + d) % times) for t in range(times)] for d in range(times)]
    raws = [lax.ppermute(trajectory, "tm", shifts[d]) for d in range(1, times)]

    xs, ys = pl.pallas_call(
        functools.partial(pack_kernel, fields),
        out_shape=(near(2 * fields, HALO, width), near(rows, LANES)),
        name="pack_edges",
    )(*kept(packs, zr_even, zr_odd))

    even, odd = (pair_up("gx", False), pair_up("gx", True))
    x_rows = [lax.ppermute(xs, "tm", shifts[d]) for d in range(1, times)]
    packs = [lax.ppermute(ys, "gx", even), lax.ppermute(ys, "gx", odd)]
    for d in range(1, times):
        packs.append(lax.ppermute(ys, ("tm", "gx"), with_steps("gx", even, d)))
        packs.append(lax.ppermute(ys, ("tm", "gx"), with_steps("gx", odd, d)))

    def dealt_out(count, tiles):
        return vmem(count, rows // SUBLANES, tiles, SUBLANES, LANES)

    def working(outputs, scratch, tiles):
        state = vmem(2, outputs, 3, rows // SUBLANES, tiles, SUBLANES, LANES)
        return [dealt_out(known, tiles), state, vmem(scratch, tiles, rows, LANES)]

    strips, part, part_residual = pl.pallas_call(
        functools.partial(block_kernel, times, steps, lags),
        out_shape=(
            near(known + 3, rows, LANES),
            near(steps, 3, rows_lat, width),
            near(steps, 3, rows_lat, width),
        ),
        scratch_shapes=[vmem(known + 3, across, rows, LANES)] + working(steps, 2 * fields, across),
        name="block_part",
    )(*kept(own, zr_even, zr_odd, *(each for both in zip(raws, x_rows) for each in both)))
    updated, residual = pl.pallas_call(
        functools.partial(rim_kernel, times, steps, lags),
        out_shape=(hbm(steps, 3, rows_lat, width), hbm(steps, 3, rows_lat, width)),
        scratch_shapes=[vmem(known + 3, 1, rows, LANES)] + working(1, fields, 1),
        name="rim_part",
    )(*kept(own, strips, part, part_residual, *packs))
    return updated, residual


def solution(mesh):
    in_specs = (P("tm", None, "gy", "gx"), P(None, "gy", "gx"))
    out_specs = (P("tm", None, "gy", "gx"), P("tm", None, "gy", "gx"))
    return jax.shard_map(step, mesh=mesh, in_specs=in_specs, out_specs=out_specs, check_vma=False)
```

profile of v0, /device:TPU:0, one launch (start us, length us, event | category | flops | bytes accessed | tf_op | source)
XLA Modules:
  0.0 23.3 jit_solution(17601170567249274171)
XLA Ops:
  0.6 3.0 %collective-permute-start.2 = (f32[2,3,32,256]{3,2,1,0:T(8,128)}, f32[2,3,32,256]{3,2,1,0:T(8,128)S(1)}, u32[]{:S(2)}, u32[]{:S(2)}) collective-permute-start(f32[2,3,32,256]{3,2,1,0:T(8,128)} %traj.1), channel_id=1, source_target_pairs={{0,16},{16,0},{1,17},{17,1},{2,18},{18,2},{3,19},{19,3},{4,20},{20... | collective-permute-start | bytes 589832 | tf_op jit(solution)/shard_map/ppermute | solution.py:378
  3.7 1.1 %split_edges.1 = (f32[9,32,256]{2,1,0:T(8,128)S(1)}, f32[9,8,256]{2,1,0:T(8,128)S(1)}, f32[9,8,256]{2,1,0:T(8,128)S(1)}, f32[32,128]{1,0:T(8,128)S(1)}) custom-call(f32[2,3,32,256]{3,2,1,0:T(8,128)} %traj.1, f32[3,32,256]{2,1,0:T(8,128)} %init.1), custom_call_target="tpu_custom_call" | custom-call | tf_op jit(solution)/shard_map/split_edges/pallas_call | solution.py:365
  4.8 1.6 %collective-permute-start = (f32[9,8,256]{2,1,0:T(8,128)S(1)}, f32[9,8,256]{2,1,0:T(8,128)S(1)}, u32[]{:S(2)}, u32[]{:S(2)}) collective-permute-start(f32[9,8,256]{2,1,0:T(8,128)S(1)} %get-tuple-element.12), channel_id=1, source_target_pairs={{0,1},{1,0},{2,3},{3,2},{4,5},{5,4},{6,7},{7,6},{8,9},{9,8},{10,11... | collective-permute-start | bytes 221192 | tf_op jit(solution)/shard_map/ppermute | solution.py:376
  6.4 2.5 %collective-permute-start.1 = (f32[9,8,256]{2,1,0:T(8,128)S(1)}, f32[9,8,256]{2,1,0:T(8,128)S(1)}, u32[]{:S(2)}, u32[]{:S(2)}) collective-permute-start(f32[9,8,256]{2,1,0:T(8,128)S(1)} %get-tuple-element.13), channel_id=1, source_target_pairs={{1,2},{2,1},{3,0},{0,3},{5,6},{6,5},{7,4},{4,7},{9,10},{10,9},{11,... | collective-permute-start | bytes 221192 | tf_op jit(solution)/shard_map/ppermute | solution.py:375
  8.9 0.3 %collective-permute-done.zr_even = f32[9,8,256]{2,1,0:T(8,128)S(1)} collective-permute-done((f32[9,8,256]{2,1,0:T(8,128)S(1)}, f32[9,8,256]{2,1,0:T(8,128)S(1)}, u32[]{:S(2)}, u32[]{:S(2)}) %collective-permute-start) | collective-permute-done | bytes 73760 | tf_op jit(solution)/shard_map/ppermute | solution.py:376
  9.2 3.4 %collective-permute-done.1.zr_odd = f32[9,8,256]{2,1,0:T(8,128)S(1)} collective-permute-done((f32[9,8,256]{2,1,0:T(8,128)S(1)}, f32[9,8,256]{2,1,0:T(8,128)S(1)}, u32[]{:S(2)}, u32[]{:S(2)}) %collective-permute-start.1) | collective-permute-done | bytes 73760 | tf_op jit(solution)/shard_map/ppermute | solution.py:375
  12.6 0.1 pack_edges.1
  12.7 0.6 %collective-permute-start.3 = (f32[12,8,256]{2,1,0:T(8,128)S(1)}, f32[12,8,256]{2,1,0:T(8,128)S(1)}, u32[]{:S(2)}, u32[]{:S(2)}) collective-permute-start(f32[12,8,256]{2,1,0:T(8,128)S(1)} %get-tuple-element.15), channel_id=1, source_target_pairs={{0,16},{16,0},{1,17},{17,1},{2,18},{18,2},{3,19},{19,3},{4,20},{20... | collective-permute-start | bytes 294920 | tf_op jit(solution)/shard_map/ppermute | solution.py:387
  13.3 0.0 collective-permute-start.4
  13.3 1.6 %collective-permute-start.5 = (f32[48,128]{1,0:T(8,128)S(1)}, f32[48,128]{1,0:T(8,128)S(1)}, u32[]{:S(2)}, u32[]{:S(2)}) collective-permute-start(f32[48,128]{1,0:T(8,128)S(1)} %get-tuple-element.19), channel_id=1, source_target_pairs={{4,8},{8,4},{12,0},{0,12},{5,9},{9,5},{13,1},{1,13},{6,10},{10,6},... | collective-permute-start | bytes 73736 | tf_op jit(solution)/shard_map/ppermute | solution.py:388
  14.9 1.1 %collective-permute-start.6 = (f32[48,128]{1,0:T(8,128)S(1)}, f32[48,128]{1,0:T(8,128)S(1)}, u32[]{:S(2)}, u32[]{:S(2)}) collective-permute-start(f32[48,128]{1,0:T(8,128)S(1)} %get-tuple-element.19), channel_id=1, source_target_pairs={{0,20},{4,16},{8,28},{12,24},{16,4},{20,0},{24,12},{28,8},{1,21},{... | collective-permute-start | bytes 73736 | tf_op jit(solution)/shard_map/ppermute | solution.py:390
  16.0 1.3 %collective-permute-done.3.refs_1_ = f32[12,8,256]{2,1,0:T(8,128)S(1)} collective-permute-done((f32[12,8,256]{2,1,0:T(8,128)S(1)}, f32[12,8,256]{2,1,0:T(8,128)S(1)}, u32[]{:S(2)}, u32[]{:S(2)}) %collective-permute-start.3) | collective-permute-done | bytes 98336 | tf_op jit(solution)/shard_map/ppermute | solution.py:387
  17.4 0.0 collective-permute-start.7
  17.4 0.0 collective-permute-done.2.refs_0_
  17.4 1.5 %block_part.1 = (f32[15,48,128]{2,1,0:T(8,128)S(1)}, f32[2,3,32,256]{3,2,1,0:T(8,128)S(1)}, f32[2,3,32,256]{3,2,1,0:T(8,128)S(1)}) custom-call(f32[9,32,256]{2,1,0:T(8,128)S(1)} %get-tuple-element.11.own, f32[9,8,256]{2,1,0:T(8,128)S(1)} %collective-permute-done.zr_even, f32[9,8,256]{2,1,0:T(8,128)S(1)} %collective-permute-done.1.zr_odd, ...), custom_call_target="tpu_custom_call" | custom-call | tf_op jit(solution)/shard_map/block_part/pallas_call | solution.py:400
  18.9 0.0 collective-permute-done.4.yr_even
  18.9 0.0 collective-permute-done.5.yr_odd
  18.9 0.0 collective-permute-done.6.refs_0_
  18.9 2.6 %collective-permute-done.7.refs_1_ = f32[48,128]{1,0:T(8,128)S(1)} collective-permute-done((f32[48,128]{1,0:T(8,128)S(1)}, f32[48,128]{1,0:T(8,128)S(1)}, u32[]{:S(2)}, u32[]{:S(2)}) %collective-permute-start.7) | collective-permute-done | bytes 24608 | tf_op jit(solution)/shard_map/ppermute | solution.py:391
  21.5 1.7 %rim_part.1 = (f32[2,3,32,256]{3,2,1,0:T(8,128)}, f32[2,3,32,256]{3,2,1,0:T(8,128)}) custom-call(f32[9,32,256]{2,1,0:T(8,128)S(1)} %get-tuple-element.11.own, f32[15,48,128]{2,1,0:T(8,128)S(1)} %get-tuple-element.16.strips, f32[2,3,32,256]{3,2,1,0:T(8,128)S(1)} %get-tuple-element.17.part, f32[2,3,32,256]{3,2,1,0:T(8,128)S(1)} %get-tuple-element.18.part_residual, ...), custom_call_target="tpu_custom_call" | custom-call | tf_op jit(solution)/shard_map/rim_part/pallas_call | solution.py:410
Async XLA Ops:
  0.6 16.8 %collective-permute-start.2 = (f32[2,3,32,256]{3,2,1,0:T(8,128)}, f32[2,3,32,256]{3,2,1,0:T(8,128)S(1)}, u32[]{:S(2)}, u32[]{:S(2)}) collective-permute-start(f32[2,3,32,256]{3,2,1,0:T(8,128)} %traj.1), channel_id=1, source_target_pairs={{0,16},{16,0},{1,17},{17,1},{2,18},{18,2},{3,19},{19,3},{4,20},{20... | collective-permute-start | bytes 589832 | tf_op jit(solution)/shard_map/ppermute | solution.py:378
  4.8 4.4 %collective-permute-start = (f32[9,8,256]{2,1,0:T(8,128)S(1)}, f32[9,8,256]{2,1,0:T(8,128)S(1)}, u32[]{:S(2)}, u32[]{:S(2)}) collective-permute-start(f32[9,8,256]{2,1,0:T(8,128)S(1)} %get-tuple-element.12), channel_id=1, source_target_pairs={{0,1},{1,0},{2,3},{3,2},{4,5},{5,4},{6,7},{7,6},{8,9},{9,8},{10,11... | collective-permute-start | bytes 221192 | tf_op jit(solution)/shard_map/ppermute | solution.py:376
  6.4 6.2 %collective-permute-start.1 = (f32[9,8,256]{2,1,0:T(8,128)S(1)}, f32[9,8,256]{2,1,0:T(8,128)S(1)}, u32[]{:S(2)}, u32[]{:S(2)}) collective-permute-start(f32[9,8,256]{2,1,0:T(8,128)S(1)} %get-tuple-element.13), channel_id=1, source_target_pairs={{1,2},{2,1},{3,0},{0,3},{5,6},{6,5},{7,4},{4,7},{9,10},{10,9},{11,... | collective-permute-start | bytes 221192 | tf_op jit(solution)/shard_map/ppermute | solution.py:375
  12.7 4.7 %collective-permute-start.3 = (f32[12,8,256]{2,1,0:T(8,128)S(1)}, f32[12,8,256]{2,1,0:T(8,128)S(1)}, u32[]{:S(2)}, u32[]{:S(2)}) collective-permute-start(f32[12,8,256]{2,1,0:T(8,128)S(1)} %get-tuple-element.15), channel_id=1, source_target_pairs={{0,16},{16,0},{1,17},{17,1},{2,18},{18,2},{3,19},{19,3},{4,20},{20... | collective-permute-start | bytes 294920 | tf_op jit(solution)/shard_map/ppermute | solution.py:387
  13.3 5.6 %collective-permute-start.4 = (f32[48,128]{1,0:T(8,128)S(1)}, f32[48,128]{1,0:T(8,128)S(1)}, u32[]{:S(2)}, u32[]{:S(2)}) collective-permute-start(f32[48,128]{1,0:T(8,128)S(1)} %get-tuple-element.19), channel_id=1, source_target_pairs={{0,4},{4,0},{8,12},{12,8},{1,5},{5,1},{9,13},{13,9},{2,6},{6,2},{1... | collective-permute-start | bytes 73736 | tf_op jit(solution)/shard_map/ppermute | solution.py:388
  13.3 5.6 %collective-permute-start.5 = (f32[48,128]{1,0:T(8,128)S(1)}, f32[48,128]{1,0:T(8,128)S(1)}, u32[]{:S(2)}, u32[]{:S(2)}) collective-permute-start(f32[48,128]{1,0:T(8,128)S(1)} %get-tuple-element.19), channel_id=1, source_target_pairs={{4,8},{8,4},{12,0},{0,12},{5,9},{9,5},{13,1},{1,13},{6,10},{10,6},... | collective-permute-start | bytes 73736 | tf_op jit(solution)/shard_map/ppermute | solution.py:388
  14.9 4.0 %collective-permute-start.6 = (f32[48,128]{1,0:T(8,128)S(1)}, f32[48,128]{1,0:T(8,128)S(1)}, u32[]{:S(2)}, u32[]{:S(2)}) collective-permute-start(f32[48,128]{1,0:T(8,128)S(1)} %get-tuple-element.19), channel_id=1, source_target_pairs={{0,20},{4,16},{8,28},{12,24},{16,4},{20,0},{24,12},{28,8},{1,21},{... | collective-permute-start | bytes 73736 | tf_op jit(solution)/shard_map/ppermute | solution.py:390
  17.4 4.2 %collective-permute-start.7 = (f32[48,128]{1,0:T(8,128)S(1)}, f32[48,128]{1,0:T(8,128)S(1)}, u32[]{:S(2)}, u32[]{:S(2)}) collective-permute-start(f32[48,128]{1,0:T(8,128)S(1)} %get-tuple-element.19), channel_id=1, source_target_pairs={{4,24},{8,20},{12,16},{0,28},{20,8},{24,4},{28,0},{16,12},{5,25},{... | collective-permute-start | bytes 73736 | tf_op jit(solution)/shard_map/ppermute | solution.py:391
where the time goes:
time: 23.4 us; the launch traced here: 23.3 us
  starting transfers between devices  10.5 us (45%)
  waiting for transfers between devices  7.66 us (33%)
  Pallas kernels  4.43 us (19%)
  between operations  0.68 us (3%)
    ppermute x1, waiting for transfers between devices, step(): zr_odd = lax.ppermute(zs_odd, 'gy', pair_up('gy', True))  3.37 us
    ppermute x1, starting transfers between devices, step(): raws = [lax.ppermute(trajectory, 'tm', shifts[d]) for d in range(1, times)]  3.03 us
    ppermute x1, waiting for transfers between devices, step(): packs.append(lax.ppermute(ys, ('tm', 'gx'), with_steps('gx', odd, d)))  2.63 us
    ppermute x1, starting transfers between devices, step(): zr_odd = lax.ppermute(zs_odd, 'gy', pair_up('gy', True))  2.47 us
    pallas_call x1, Pallas kernels, step(): pl.pallas_call(functools.partial(rim_kernel, times, steps, lags), out_sha...  1.71 us
    ppermute x1, starting transfers between devices, step(): zr_even = lax.ppermute(zs_even, 'gy', pair_up('gy', False))  1.64 us
    ppermute x2, starting transfers between devices, step(): packs = [lax.ppermute(ys, 'gx', even), lax.ppermute(ys, 'gx', odd)]  1.63 us
    pallas_call x1, Pallas kernels, step(): pl.pallas_call(functools.partial(block_kernel, times, steps, lags), out_s...  1.48 us
  transfers between devices with their start and end apart: 8, of which 4 were waited for; matrix products, arithmetic and copies ran while one was open for 0% of the time, Pallas kernels for 12%

commit v1 on v0

--- a/solution.py
+++ b/solution.py
@@ -101,26 +101,51 @@
     return packed
 
 
-def split_kernel(fields, traj, init, own, zs_even, zs_odd, packs):
+def edge_kernel(steps, traj, init, zs_even, zs_odd, sems):
+    rows_lat = traj.shape[-2]
+    gy_even = lax.axis_index("gy") % 2 == 0
+    copies = []
+    for side, (target, south) in enumerate(((zs_even, gy_even), (zs_odd, jnp.logical_not(gy_even)))):
+        rows = pl.ds(pl.multiple_of(jnp.where(south, rows_lat - HALO, 0), SUBLANES), HALO)
+        for l in range(steps + 1):
+            source = traj.at[l, :, rows, :] if l < steps else init.at[:, rows, :]
+            copies.append(pltpu.make_async_copy(source, target.at[pl.ds(3 * l, 3)], sems.at[side, l]))
+    for copy in copies:
+        copy.start()
+    for copy in copies:
+        copy.wait()
+
+
+def split_kernel(fields, traj, init, own, packs):
     rows_lat, width = traj.shape[-2:]
-    gy_even = lax.axis_index("gy") % 2 == 0
     for f in range(fields + 3):
-        field = traj[f // 3, f % 3] if f < fields else init[f - fields]
-        own[f] = field
-        north, south = (field[:HALO], field[rows_lat - HALO :])
-        zs_even[f] = jnp.where(gy_even, south, north)
-        zs_odd[f] = jnp.where(gy_even, north, south)
+        own[f] = traj[f // 3, f % 3] if f < fields else init[f - fields]
     for rows in range(rows_lat // SUBLANES):
         at = pl.ds(rows * SUBLANES, SUBLANES)
         packs[at, :] = gather_columns([own.at[f, at] for f in range(fields + 3)], width)
 
 
-def pack_kernel(fields, packs, zr_even, zr_odd, xs, ys):
+def other_pack_kernel(fields, *refs):
+    own, others, packs = refs[0], refs[1:-1], refs[-1]
+    gy_even = lax.axis_index("gy") % 2 == 0
+    packs[0] = own[...]
+    for d in range(len(others) // 3):
+        raw, xr_even, xr_odd = others[3 * d : 3 * d + 3]
+        rows_lat, width = raw.shape[-2:]
+        even = gather_columns([xr_even.at[f] for f in range(fields)], width)
+        odd = gather_columns([xr_odd.at[f] for f in range(fields)], width)
+        packs[d + 1, :HALO, :] = jnp.where(gy_even, odd, even)
+        packs[d + 1, HALO + rows_lat :, :] = jnp.where(gy_even, even, odd)
+        for rows in range(rows_lat // SUBLANES):
+            at = pl.ds(rows * SUBLANES, SUBLANES)
+            tiles = [raw.at[f // 3, f % 3, at] for f in range(fields)]
+            packs[d + 1, pl.ds(HALO + rows * SUBLANES, SUBLANES), :] = gather_columns(tiles, width)
+
+
+def pack_kernel(fields, packs, zr_even, zr_odd, ys):
     width = zr_even.shape[-1]
     gy_even = lax.axis_index("gy") % 2 == 0
     rows_lat = packs.shape[0]
-    xs[:fields] = zr_even[:fields]
-    xs[fields:] = zr_odd[:fields]
     even = gather_columns([zr_even.at[f] for f in range(fields + 3)], width)
     odd = gather_columns([zr_odd.at[f] for f in range(fields + 3)], width)
     ys[:HALO, :] = jnp.where(gy_even, odd, even)
@@ -272,14 +297,14 @@
 
 def block_kernel(times, steps, lags, own, zr_even, zr_odd, *refs):
     fields = 3 * steps
-    others = refs[: 2 * (times - 1)]
-    strips, part, residual, ext, rates, state, scratch = refs[2 * (times - 1) :]
+    others = refs[: 3 * (times - 1)]
+    strips, part, residual, ext, rates, state, scratch = refs[3 * (times - 1) :]
     rows_lat = own.shape[-2]
     place(ext, 0, [own.at[f] for f in range(fields)], zr_even.at[:fields], zr_odd.at[:fields])
     for d in range(1, times):
-        raw, xr = others[2 * (d - 1) : 2 * d]
+        raw, xr_even, xr_odd = others[3 * (d - 1) : 3 * d]
         blocks = [raw.at[f // 3, f % 3] for f in range(fields)]
-        place(ext, d * fields, blocks, xr.at[:fields], xr.at[fields:])
+        place(ext, d * fields, blocks, xr_even, xr_odd)
     place(ext, times * fields, [own.at[fields + c] for c in range(3)], zr_even.at[fields:], zr_odd.at[fields:])
     rotation = [coriolis(q, rows_lat) for q in range(rates.shape[1])]
     residuals(times, steps, ext, rates, rotation, lambda l, c, q, values: put(scratch, 3 * l + c, q, values))
@@ -300,14 +325,13 @@
 
 def rim_kernel(times, steps, lags, own, strips, part, part_residual, yr_even, yr_odd, *refs):
     fields, half = 3 * steps, LANES // 2
-    packs = refs[: 2 * (times - 1)]
-    updated, residual, rim, rates, state, scratch = refs[2 * (times - 1) :]
+    updated, residual, rim, rates, state, scratch, ready, sems = refs[times - 1 :]
     rows_lat, width = own.shape[-2:]
     tiles = rates.shape[1]
-    place_rim(rim, strips, 0, fields, 0, yr_even, yr_odd)
-    place_rim(rim, strips, times * fields, 3, fields, yr_even, yr_odd)
+    place_rim(rim, strips, 0, fields, 0, yr_even.at[0], yr_odd)
+    place_rim(rim, strips, times * fields, 3, fields, yr_even.at[0], yr_odd)
     for d in range(1, times):
-        place_rim(rim, strips, d * fields, fields, 0, *packs[2 * (d - 1) : 2 * d])
+        place_rim(rim, strips, d * fields, fields, 0, yr_even.at[d], refs[d - 1])
     rotation = [coriolis(q, rows_lat) for q in range(tiles)]
     residuals(times, steps, rim, rates, rotation, lambda l, c, q, values: put(scratch, 3 * l + c, q, values))
     lane = lax.broadcasted_iota(jnp.int32, (rows_lat, LANES), 1)
@@ -320,9 +344,12 @@
         value[-1] = jnp.where(lane >= LANES - REACH, tail, value[-1])
         return jnp.concatenate(value, axis=1)
 
+    copies = []
     for l in range(steps):
         for c in range(3):
-            residual[l, c] = merged(part_residual[l, c], block_of(scratch, 3 * l + c, rows_lat), 0)
+            ready[l, c] = merged(part_residual[l, c], block_of(scratch, 3 * l + c, rows_lat), 0)
+            copies.append(pltpu.make_async_copy(ready.at[l, c], residual.at[l, c], sems.at[l, c]))
+            copies[-1].start()
 
     second = within(LANES - 2 * REACH, 3 * REACH, APART) | within(half, 3 * REACH, APART)
     for f in range(times * fields):
@@ -338,7 +365,11 @@
         for c in range(3):
             strip = block_of(scratch, c, rows_lat)
             for m in range(n, min(n + 2, steps)):
-                updated[m, c] = own[3 * m + c] - merged(part[m, c], strip, (m - n) * APART)
+                ready[steps + m, c] = own[3 * m + c] - merged(part[m, c], strip, (m - n) * APART)
+                copies.append(pltpu.make_async_copy(ready.at[steps + m, c], updated.at[m, c], sems.at[steps + m, c]))
+                copies[-1].start()
+    for copy in copies:
+        copy.wait()
 
 
 def step(trajectory, initial):
@@ -362,33 +393,41 @@
     def kept(*arrays):
         return [pltpu.with_memory_space_constraint(array, pltpu.VMEM) if fits else array for array in arrays]
 
-    own, zs_even, zs_odd, packs = pl.pallas_call(
-        functools.partial(split_kernel, fields),
-        out_shape=(
-            near(fields + 3, rows_lat, width),
-            near(fields + 3, HALO, width),
-            near(fields + 3, HALO, width),
-            near(rows_lat, LANES),
-        ),
-        name="split_edges",
+    zs_even, zs_odd = pl.pallas_call(
+        functools.partial(edge_kernel, steps),
+        in_specs=[pl.BlockSpec(memory_space=pl.ANY)] * 2,
+        out_shape=(near(fields + 3, HALO, width), near(fields + 3, HALO, width)),
+        scratch_shapes=[pltpu.SemaphoreType.DMA((2, steps + 1))],
+        name="edge_rows",
     )(trajectory, initial)
     zr_odd = lax.ppermute(zs_odd, "gy", pair_up("gy", True))
     zr_even = lax.ppermute(zs_even, "gy", pair_up("gy", False))
+    own, packs = pl.pallas_call(
+        functools.partial(split_kernel, fields),
+        out_shape=(near(fields + 3, rows_lat, width), near(rows_lat, LANES)),
+        name="split_block",
+    )(trajectory, initial)
     shifts = [[(t, (t + d) % times) for t in range(times)] for d in range(times)]
     raws = [lax.ppermute(trajectory, "tm", shifts[d]) for d in range(1, times)]
 
-    xs, ys = pl.pallas_call(
+    ys = pl.pallas_call(
         functools.partial(pack_kernel, fields),
-        out_shape=(near(2 * fields, HALO, width), near(rows, LANES)),
+        out_shape=near(rows, LANES),
         name="pack_edges",
     )(*kept(packs, zr_even, zr_odd))
 
     even, odd = (pair_up("gx", False), pair_up("gx", True))
-    x_rows = [lax.ppermute(xs, "tm", shifts[d]) for d in range(1, times)]
-    packs = [lax.ppermute(ys, "gx", even), lax.ppermute(ys, "gx", odd)]
-    for d in range(1, times):
-        packs.append(lax.ppermute(ys, ("tm", "gx"), with_steps("gx", even, d)))
-        packs.append(lax.ppermute(ys, ("tm", "gx"), with_steps("gx", odd, d)))
+    xr_even = [lax.ppermute(zr_even[:fields], "tm", shifts[d]) for d in range(1, times)]
+    xr_odd = [lax.ppermute(zr_odd[:fields], "tm", shifts[d]) for d in range(1, times)]
+    odds = [lax.ppermute(ys, ("tm", "gx"), with_steps("gx", odd, d)) for d in range(1, times)]
+    odds.insert(0, lax.ppermute(ys, "gx", odd))
+    known_of = [each for both in zip(raws, xr_even, xr_odd) for each in both]
+    ys_all = pl.pallas_call(
+        functools.partial(other_pack_kernel, fields),
+        out_shape=near(times, rows, LANES),
+        name="pack_others",
+    )(*kept(ys, *known_of))
+    evens = lax.ppermute(ys_all, "gx", even)
 
     def dealt_out(count, tiles):
         return vmem(count, rows // SUBLANES, tiles, SUBLANES, LANES)
@@ -406,13 +445,19 @@
         ),
         scratch_shapes=[vmem(known + 3, across, rows, LANES)] + working(steps, 2 * fields, across),
         name="block_part",
-    )(*kept(own, zr_even, zr_odd, *(each for both in zip(raws, x_rows) for each in both)))
+    )(*kept(own, zr_even, zr_odd, *known_of))
     updated, residual = pl.pallas_call(
         functools.partial(rim_kernel, times, steps, lags),
         out_shape=(hbm(steps, 3, rows_lat, width), hbm(steps, 3, rows_lat, width)),
-        scratch_shapes=[vmem(known + 3, 1, rows, LANES)] + working(1, fields, 1),
+        out_specs=(pl.BlockSpec(memory_space=pl.ANY),) * 2,
+        scratch_shapes=[
+            vmem(known + 3, 1, rows, LANES),
+            *working(1, fields, 1),
+            vmem(2 * steps, 3, rows_lat, width),
+            pltpu.SemaphoreType.DMA((2 * steps, 3)),
+        ],
         name="rim_part",
-    )(*kept(own, strips, part, part_residual, *packs))
+    )(*kept(own, strips, part, part_residual, evens, *odds))
     return updated, residual
 
 

time: 23.4 us -> 24.4 us (1.043)
  Pallas kernels: 4.43 us -> 5.44 us
  starting transfers between devices: 10.5 us -> 9.83 us
  waiting for transfers between devices: 7.66 us -> 8.2 us
    pallas_call x1 -> x3, Pallas kernels: 0.1 us -> 1.11 us  [the longest x1 0.87 us: step(): pl.pallas_call(functools.partial(edge_kernel, steps), in_specs=[pl.BlockS...]
    ppermute x5, waiting for transfers between devices: 3.99 us -> 4.82 us  [the longest x1 2.45 us: step(): lax.ppermute(ys, ('tm', 'gx'), with_steps('gx', odd, d))]
    ppermute x5, starting transfers between devices: 3.34 us -> 2.68 us  [the longest x1 1.62 us: step(): odds.insert(0, lax.ppermute(ys, 'gx', odd))]
    ppermute x1, waiting for transfers between devices: 3.37 us -> 3.07 us  [step(): zr_odd = lax.ppermute(zs_odd, 'gy', pair_up('gy', True))]
  transfers between devices with their start and end apart: 8 -> 8, of which waited for: 4 -> 5; matrix products, arithmetic and copies ran while one was open for 0% -> 0% of each run, Pallas kernels for 12% -> 15%
where the time goes in v1:
time: 24.4 us; the launch traced here: 24.1 us
  starting transfers between devices  9.83 us (40%)
  waiting for transfers between devices  8.2 us (34%)
  Pallas kernels  5.44 us (22%)
  between operations  0.67 us (3%)
    ppermute x1, waiting for transfers between devices, step(): zr_odd = lax.ppermute(zs_odd, 'gy', pair_up('gy', True))  3.07 us
    ppermute x1, starting transfers between devices, step(): raws = [lax.ppermute(trajectory, 'tm', shifts[d]) for d in range(1, times)]  3.03 us
    ppermute x1, starting transfers between devices, step(): zr_odd = lax.ppermute(zs_odd, 'gy', pair_up('gy', True))  2.47 us
    ppermute x1, waiting for transfers between devices, step(): lax.ppermute(ys, ('tm', 'gx'), with_steps('gx', odd, d))  2.45 us
    ppermute x1, waiting for transfers between devices, step(): lax.ppermute(zr_odd[:fields], 'tm', shifts[d])  2.31 us
    pallas_call x1, Pallas kernels, step(): pl.pallas_call(functools.partial(rim_kernel, times, steps, lags), out_sha...  1.72 us
    ppermute x1, starting transfers between devices, step(): zr_even = lax.ppermute(zs_even, 'gy', pair_up('gy', False))  1.64 us
    ppermute x1, starting transfers between devices, step(): odds.insert(0, lax.ppermute(ys, 'gx', odd))  1.62 us
  transfers between devices with their start and end apart: 8, of which 5 were waited for; matrix products, arithmetic and copies ran while one was open for 0% of the time, Pallas kernels for 15%

profile of v1, /device:TPU:0, one launch (start us, length us, event | category | flops | bytes accessed | tf_op | source)
XLA Modules:
  0.0 24.1 jit_solution(14071492695270020648)
XLA Ops:
  0.6 3.0 %collective-permute-start.2 = (f32[2,3,32,256]{3,2,1,0:T(8,128)}, f32[2,3,32,256]{3,2,1,0:T(8,128)S(1)}, u32[]{:S(2)}, u32[]{:S(2)}) collective-permute-start(f32[2,3,32,256]{3,2,1,0:T(8,128)} %traj.3), channel_id=1, source_target_pairs={{0,16},{16,0},{1,17},{17,1},{2,18},{18,2},{3,19},{19,3},{4,20},{20... | collective-permute-start | bytes 589832 | tf_op jit(solution)/shard_map/ppermute | solution.py:411
  3.7 0.9 %edge_rows.1 = (f32[9,8,256]{2,1,0:T(8,128)S(1)}, f32[9,8,256]{2,1,0:T(8,128)S(1)}) custom-call(f32[2,3,32,256]{3,2,1,0:T(8,128)} %traj.3, f32[3,32,256]{2,1,0:T(8,128)} %init.3), custom_call_target="tpu_custom_call" | custom-call | tf_op jit(solution)/shard_map/edge_rows/pallas_call | solution.py:396
  4.5 1.6 %collective-permute-start = (f32[9,8,256]{2,1,0:T(8,128)S(1)}, f32[9,8,256]{2,1,0:T(8,128)S(1)}, u32[]{:S(2)}, u32[]{:S(2)}) collective-permute-start(f32[9,8,256]{2,1,0:T(8,128)S(1)} %get-tuple-element.10), channel_id=1, source_target_pairs={{0,1},{1,0},{2,3},{3,2},{4,5},{5,4},{6,7},{7,6},{8,9},{9,8},{10,11... | collective-permute-start | bytes 221192 | tf_op jit(solution)/shard_map/ppermute | solution.py:404
  6.2 2.5 %collective-permute-start.1 = (f32[9,8,256]{2,1,0:T(8,128)S(1)}, f32[9,8,256]{2,1,0:T(8,128)S(1)}, u32[]{:S(2)}, u32[]{:S(2)}) collective-permute-start(f32[9,8,256]{2,1,0:T(8,128)S(1)} %get-tuple-element.11), channel_id=1, source_target_pairs={{1,2},{2,1},{3,0},{0,3},{5,6},{6,5},{7,4},{4,7},{9,10},{10,9},{11,... | collective-permute-start | bytes 221192 | tf_op jit(solution)/shard_map/ppermute | solution.py:403
  8.7 0.3 %collective-permute-done.zr_even = f32[9,8,256]{2,1,0:T(8,128)S(1)} collective-permute-done((f32[9,8,256]{2,1,0:T(8,128)S(1)}, f32[9,8,256]{2,1,0:T(8,128)S(1)}, u32[]{:S(2)}, u32[]{:S(2)}) %collective-permute-start) | collective-permute-done | bytes 73760 | tf_op jit(solution)/shard_map/ppermute | solution.py:404
  9.0 0.3 %collective-permute-start.3 = (f32[6,8,256]{2,1,0:T(8,128)S(1)}, f32[6,8,256]{2,1,0:T(8,128)S(1)}, u32[]{:S(2)}, u32[]{:S(2)}) collective-permute-start(f32[6,8,256]{2,1,0:T(8,128)S(1)} %slice.8), channel_id=1, source_target_pairs={{0,16},{16,0},{1,17},{17,1},{2,18},{18,2},{3,19},{19,3},{4,20},{20... | collective-permute-start | bytes 147464 | tf_op jit(solution)/shard_map/ppermute | solution.py:420
  9.3 3.1 %collective-permute-done.1.zr_odd = f32[9,8,256]{2,1,0:T(8,128)S(1)} collective-permute-done((f32[9,8,256]{2,1,0:T(8,128)S(1)}, f32[9,8,256]{2,1,0:T(8,128)S(1)}, u32[]{:S(2)}, u32[]{:S(2)}) %collective-permute-start.1) | collective-permute-done | bytes 73760 | tf_op jit(solution)/shard_map/ppermute | solution.py:403
  12.3 0.5 %collective-permute-start.4 = (f32[6,8,256]{2,1,0:T(8,128)S(1)}, f32[6,8,256]{2,1,0:T(8,128)S(1)}, u32[]{:S(2)}, u32[]{:S(2)}) collective-permute-start(f32[6,8,256]{2,1,0:T(8,128)S(1)} %slice.9), channel_id=1, source_target_pairs={{0,16},{16,0},{1,17},{17,1},{2,18},{18,2},{3,19},{19,3},{4,20},{20... | collective-permute-start | bytes 147464 | tf_op jit(solution)/shard_map/ppermute | solution.py:421
  12.9 1.1 %split_block.1 = (f32[9,32,256]{2,1,0:T(8,128)S(1)}, f32[32,128]{1,0:T(8,128)S(1)}) custom-call(f32[2,3,32,256]{3,2,1,0:T(8,128)} %traj.3, f32[3,32,256]{2,1,0:T(8,128)} %init.3), custom_call_target="tpu_custom_call" | custom-call | tf_op jit(solution)/shard_map/split_block/pallas_call | solution.py:405
  14.0 0.1 pack_edges.1.refs_0_
  14.1 0.0 collective-permute-done.3.refs_1_.refs_2_
  14.1 2.3 %collective-permute-done.4.refs_2_.refs_3_ = f32[6,8,256]{2,1,0:T(8,128)S(1)} collective-permute-done((f32[6,8,256]{2,1,0:T(8,128)S(1)}, f32[6,8,256]{2,1,0:T(8,128)S(1)}, u32[]{:S(2)}, u32[]{:S(2)}) %collective-permute-start.4) | collective-permute-done | bytes 49184 | tf_op jit(solution)/shard_map/ppermute | solution.py:421
  16.4 0.0 collective-permute-done.2.refs_0_.refs_1_
  16.4 0.1 pack_others.1
  16.6 0.1 collective-permute-start.5
  16.7 1.6 %collective-permute-start.6 = (f32[48,128]{1,0:T(8,128)S(1)}, f32[48,128]{1,0:T(8,128)S(1)}, u32[]{:S(2)}, u32[]{:S(2)}) collective-permute-start(f32[48,128]{1,0:T(8,128)S(1)} %pack_edges.1.refs_0_), channel_id=1, source_target_pairs={{4,8},{8,4},{12,0},{0,12},{5,9},{9,5},{13,1},{1,13},{6,10},{10,6},... | collective-permute-start | bytes 73736 | tf_op jit(solution)/shard_map/ppermute | solution.py:423
  18.3 0.2 collective-permute-start.7
  18.4 1.5 %block_part.1 = (f32[15,48,128]{2,1,0:T(8,128)S(1)}, f32[2,3,32,256]{3,2,1,0:T(8,128)S(1)}, f32[2,3,32,256]{3,2,1,0:T(8,128)S(1)}) custom-call(f32[9,32,256]{2,1,0:T(8,128)S(1)} %get-tuple-element.9.own, f32[9,8,256]{2,1,0:T(8,128)S(1)} %collective-permute-done.zr_even, f32[9,8,256]{2,1,0:T(8,128)S(1)} %collective-permute-done.1.zr_odd, ...), custom_call_target="tpu_custom_call" | custom-call | tf_op jit(solution)/shard_map/block_part/pallas_call | solution.py:439
  19.9 0.1 collective-permute-done.6.yr_odd
  20.0 2.5 %collective-permute-done.7.refs_0_ = f32[48,128]{1,0:T(8,128)S(1)} collective-permute-done((f32[48,128]{1,0:T(8,128)S(1)}, f32[48,128]{1,0:T(8,128)S(1)}, u32[]{:S(2)}, u32[]{:S(2)}) %collective-permute-start.7) | collective-permute-done | bytes 24608 | tf_op jit(solution)/shard_map/ppermute | solution.py:422
  22.4 0.0 collective-permute-done.5.yr_even
  22.4 1.7 %rim_part.1 = (f32[2,3,32,256]{3,2,1,0:T(8,128)}, f32[2,3,32,256]{3,2,1,0:T(8,128)}) custom-call(f32[9,32,256]{2,1,0:T(8,128)S(1)} %get-tuple-element.9.own, f32[15,48,128]{2,1,0:T(8,128)S(1)} %get-tuple-element.12.strips, f32[2,3,32,256]{3,2,1,0:T(8,128)S(1)} %get-tuple-element.13.part, f32[2,3,32,256]{3,2,1,0:T(8,128)S(1)} %get-tuple-element.14.part_residual, ...), custom_call_target="tpu_custom_call" | custom-call | tf_op jit(solution)/shard_map/rim_part/pallas_call | solution.py:449
  (2 shorter events, 0.0 us)
Async XLA Ops:
  0.6 15.8 %collective-permute-start.2 = (f32[2,3,32,256]{3,2,1,0:T(8,128)}, f32[2,3,32,256]{3,2,1,0:T(8,128)S(1)}, u32[]{:S(2)}, u32[]{:S(2)}) collective-permute-start(f32[2,3,32,256]{3,2,1,0:T(8,128)} %traj.3), channel_id=1, source_target_pairs={{0,16},{16,0},{1,17},{17,1},{2,18},{18,2},{3,19},{19,3},{4,20},{20... | collective-permute-start | bytes 589832 | tf_op jit(solution)/shard_map/ppermute | solution.py:411
  4.5 4.4 %collective-permute-start = (f32[9,8,256]{2,1,0:T(8,128)S(1)}, f32[9,8,256]{2,1,0:T(8,128)S(1)}, u32[]{:S(2)}, u32[]{:S(2)}) collective-permute-start(f32[9,8,256]{2,1,0:T(8,128)S(1)} %get-tuple-element.10), channel_id=1, source_target_pairs={{0,1},{1,0},{2,3},{3,2},{4,5},{5,4},{6,7},{7,6},{8,9},{9,8},{10,11... | collective-permute-start | bytes 221192 | tf_op jit(solution)/shard_map/ppermute | solution.py:404
  6.2 6.2 %collective-permute-start.1 = (f32[9,8,256]{2,1,0:T(8,128)S(1)}, f32[9,8,256]{2,1,0:T(8,128)S(1)}, u32[]{:S(2)}, u32[]{:S(2)}) collective-permute-start(f32[9,8,256]{2,1,0:T(8,128)S(1)} %get-tuple-element.11), channel_id=1, source_target_pairs={{1,2},{2,1},{3,0},{0,3},{5,6},{6,5},{7,4},{4,7},{9,10},{10,9},{11,... | collective-permute-start | bytes 221192 | tf_op jit(solution)/shard_map/ppermute | solution.py:403
  9.0 5.2 %collective-permute-start.3 = (f32[6,8,256]{2,1,0:T(8,128)S(1)}, f32[6,8,256]{2,1,0:T(8,128)S(1)}, u32[]{:S(2)}, u32[]{:S(2)}) collective-permute-start(f32[6,8,256]{2,1,0:T(8,128)S(1)} %slice.8), channel_id=1, source_target_pairs={{0,16},{16,0},{1,17},{17,1},{2,18},{18,2},{3,19},{19,3},{4,20},{20... | collective-permute-start | bytes 147464 | tf_op jit(solution)/shard_map/ppermute | solution.py:420
  12.3 4.1 %collective-permute-start.4 = (f32[6,8,256]{2,1,0:T(8,128)S(1)}, f32[6,8,256]{2,1,0:T(8,128)S(1)}, u32[]{:S(2)}, u32[]{:S(2)}) collective-permute-start(f32[6,8,256]{2,1,0:T(8,128)S(1)} %slice.9), channel_id=1, source_target_pairs={{0,16},{16,0},{1,17},{17,1},{2,18},{18,2},{3,19},{19,3},{4,20},{20... | collective-permute-start | bytes 147464 | tf_op jit(solution)/shard_map/ppermute | solution.py:421
  16.6 5.9 %collective-permute-start.5 = (f32[2,48,128]{2,1,0:T(8,128)S(1)}, f32[2,48,128]{2,1,0:T(8,128)S(1)}, u32[]{:S(2)}, u32[]{:S(2)}) collective-permute-start(f32[2,48,128]{2,1,0:T(8,128)S(1)} %pack_others.1), channel_id=1, source_target_pairs={{0,4},{4,0},{8,12},{12,8},{1,5},{5,1},{9,13},{13,9},{2,6},{6,2},{1... | collective-permute-start | bytes 147464 | tf_op jit(solution)/shard_map/ppermute | solution.py:430
  16.7 3.3 %collective-permute-start.6 = (f32[48,128]{1,0:T(8,128)S(1)}, f32[48,128]{1,0:T(8,128)S(1)}, u32[]{:S(2)}, u32[]{:S(2)}) collective-permute-start(f32[48,128]{1,0:T(8,128)S(1)} %pack_edges.1.refs_0_), channel_id=1, source_target_pairs={{4,8},{8,4},{12,0},{0,12},{5,9},{9,5},{13,1},{1,13},{6,10},{10,6},... | collective-permute-start | bytes 73736 | tf_op jit(solution)/shard_map/ppermute | solution.py:423
  18.3 4.2 %collective-permute-start.7 = (f32[48,128]{1,0:T(8,128)S(1)}, f32[48,128]{1,0:T(8,128)S(1)}, u32[]{:S(2)}, u32[]{:S(2)}) collective-permute-start(f32[48,128]{1,0:T(8,128)S(1)} %pack_edges.1.refs_0_), channel_id=1, source_target_pairs={{4,24},{8,20},{12,16},{0,28},{20,8},{24,4},{28,0},{16,12},{5,25},{... | collective-permute-start | bytes 73736 | tf_op jit(solution)/shard_map/ppermute | solution.py:422

commit v2 on v1

--- a/solution.py
+++ b/solution.py
@@ -178,7 +178,7 @@
             strips[f, rows, :] = jnp.where(within(LANES // 2 + REACH, 2 * REACH), head, ext[f, tiles - 1, rows, :])
 
 
-def place_rim(rim, strips, at, count, slot, pack_even, pack_odd):
+def place_rim(rim, base, strips, at, count, slot, pack_even, pack_odd):
     half = LANES // 2
     lane = lax.broadcasted_iota(jnp.int32, (SUBLANES, LANES), 1)
     gx_even = lax.axis_index("gx") % 2 == 0
@@ -189,7 +189,7 @@
         both = jnp.where(from_odd, pack_odd[rows, :], pack_even[rows, :])
         for f in range(count):
             value = pltpu.roll(both, half - REACH * (slot + f), 1)
-            rim[at + f, 0, rows, :] = jnp.where(outside, value, strips[at + f, rows, :])
+            rim[base + f, 0, rows, :] = jnp.where(outside, value, strips[at + f, rows, :])
 
 
 def coriolis(q, rows_lat):
@@ -219,11 +219,11 @@
     return out
 
 
-def horner(rates, weights, state, turn, write):
-    outputs, (tiles, across) = range(len(weights)), rates.shape[1:3]
+def horner(rate, weights, state, turn, write):
+    outputs, (tiles, across) = range(len(weights)), state.shape[3:5]
 
     def blend(n, j, c, q):
-        terms = lambda t: (w[j] * rates[3 * i + c, q, t] for i, w in enumerate(weights[n]))
+        terms = lambda t: (w[j] * rate(3 * i + c, q, t) for i, w in enumerate(weights[n]))
         return [functools.reduce(operator.add, terms(t)) for t in range(across)]
 
     for q in range(tiles):
@@ -295,26 +295,70 @@
     ]
 
 
-def block_kernel(times, steps, lags, own, zr_even, zr_odd, *refs):
+def own_kernel(steps, own, zr_even, zr_odd, ext, strips, rates):
+    fields = 3 * steps
+    rows_lat = own.shape[-2]
+    tiles, _ = rates.shape[1:3]
+    place(ext, 0, [own.at[f] for f in range(fields + 3)], zr_even, zr_odd)
+    place_strips(strips, ext, fields + 3)
+    rotation = [coriolis(q, rows_lat) for q in range(tiles)]
+    for l in range(steps):
+        for q in range(tiles):
+            out = tendency(lambda c, row: dealt(ext, 3 * l + c, row), q, tiles, rotation[q])
+            for c in range(3):
+                values = out[c]
+                if l:
+                    values = [a - b for a, b in zip(values, dealt(ext, 3 * (l - 1) + c, q))]
+                for t, value in enumerate(values):
+                    rates[3 * l + c, q, t] = value
+
+
+def block_kernel(times, steps, lags, ext_own, rates_own, *refs):
     fields = 3 * steps
     others = refs[: 3 * (times - 1)]
     strips, part, residual, ext, rates, state, scratch = refs[3 * (times - 1) :]
-    rows_lat = own.shape[-2]
-    place(ext, 0, [own.at[f] for f in range(fields)], zr_even.at[:fields], zr_odd.at[:fields])
+    rows_lat = ext.shape[2] - 2 * HALO
+    tiles = rates.shape[1]
     for d in range(1, times):
         raw, xr_even, xr_odd = others[3 * (d - 1) : 3 * d]
         blocks = [raw.at[f // 3, f % 3] for f in range(fields)]
-        place(ext, d * fields, blocks, xr_even, xr_odd)
-    place(ext, times * fields, [own.at[fields + c] for c in range(3)], zr_even.at[fields:], zr_odd.at[fields:])
-    rotation = [coriolis(q, rows_lat) for q in range(rates.shape[1])]
-    residuals(times, steps, ext, rates, rotation, lambda l, c, q, values: put(scratch, 3 * l + c, q, values))
+        place(ext, (d - 1) * fields, blocks, xr_even, xr_odd)
+    rotation = [coriolis(q, rows_lat) for q in range(tiles)]
+    me = lax.axis_index("tm")
+
+    def before(d, c, q):
+        last = dealt(ext_own, fields - 3 + c, q) if d + 1 == times else dealt(ext, (d + 1) * fields - 3 + c, q)
+        return [jnp.where(me == d, a, b) for a, b in zip(dealt(ext_own, fields + c, q), last)]
+
+    for q in range(tiles):
+        for f in range(fields):
+            values = [rates_own[f, q, t] for t in range(rates.shape[2])]
+            if f < 3:
+                values = [a - b for a, b in zip(values, before(0, f, q))]
+                for t, value in enumerate(values):
+                    rates[f, q, t] = value
+            put(scratch, f, q, values)
+    for d in range(1, times):
+        scale = jnp.where(me < d, jnp.float32(CIRCULANT), jnp.float32(1.0))
+        for l in range(steps):
+            at = (d - 1) * fields + 3 * l
+            for q in range(tiles):
+                out = tendency(lambda c, row: dealt(ext, at + c, row), q, tiles, rotation[q])
+                for c in range(3):
+                    prior = dealt(ext, at - 3 + c, q) if l else before(d, c, q)
+                    for t, value in enumerate(out[c]):
+                        rates[3 + at + c, q, t] = scale * (value - prior[t])
     for l in range(steps):
         for c in range(3):
             residual[l, c] = block_of(scratch, 3 * l + c, rows_lat)
-    place_strips(strips, ext, times * fields + 3)
+    place_strips(strips, ext, (times - 1) * fields)
     turn = [r * (1.0 / COURANT) for r in rotation]
     weights = weights_for(times, steps, lags)
-    horner(rates, weights, state, turn, lambda n, c, q, values: put(scratch, fields + 3 * n + c, q, values))
+
+    def rate(k, q, t):
+        return rates[k, q, t] if k < 3 else rates_own[k, q, t] if k < fields else rates[k - fields + 3, q, t]
+
+    horner(rate, weights, state, turn, lambda n, c, q, values: put(scratch, fields + 3 * n + c, q, values))
     for n in range(steps):
         for c in range(3):
             part[n, c] = block_of(scratch, fields + 3 * n + c, rows_lat)
@@ -323,15 +367,15 @@
 APART = 4 * REACH
 
 
-def rim_kernel(times, steps, lags, own, strips, part, part_residual, yr_even, yr_odd, *refs):
+def rim_kernel(times, steps, lags, own, strips_own, strips, part, part_residual, yr_even, yr_odd, *refs):
     fields, half = 3 * steps, LANES // 2
     updated, residual, rim, rates, state, scratch, ready, sems = refs[times - 1 :]
     rows_lat, width = own.shape[-2:]
     tiles = rates.shape[1]
-    place_rim(rim, strips, 0, fields, 0, yr_even.at[0], yr_odd)
-    place_rim(rim, strips, times * fields, 3, fields, yr_even.at[0], yr_odd)
+    place_rim(rim, 0, strips_own, 0, fields, 0, yr_even.at[0], yr_odd)
+    place_rim(rim, times * fields, strips_own, fields, 3, fields, yr_even.at[0], yr_odd)
     for d in range(1, times):
-        place_rim(rim, strips, d * fields, fields, 0, yr_even.at[d], refs[d - 1])
+        place_rim(rim, d * fields, strips, (d - 1) * fields, fields, 0, yr_even.at[d], refs[d - 1])
     rotation = [coriolis(q, rows_lat) for q in range(tiles)]
     residuals(times, steps, rim, rates, rotation, lambda l, c, q, values: put(scratch, 3 * l + c, q, values))
     lane = lax.broadcasted_iota(jnp.int32, (rows_lat, LANES), 1)
@@ -361,7 +405,7 @@
         pair = [
             [[jnp.where(second, b, a) for a, b in zip(*both)] for both in zip(plain[n], plain[min(n + 1, steps - 1)])]
         ]
-        horner(rates, pair, state, turn, lambda _, c, q, values: put(scratch, c, q, values))
+        horner(lambda k, q, t: rates[k, q, t], pair, state, turn, lambda _, c, q, values: put(scratch, c, q, values))
         for c in range(3):
             strip = block_of(scratch, c, rows_lat)
             for m in range(n, min(n + 2, steps)):
@@ -429,35 +473,41 @@
     )(*kept(ys, *known_of))
     evens = lax.ppermute(ys_all, "gx", even)
 
-    def dealt_out(count, tiles):
-        return vmem(count, rows // SUBLANES, tiles, SUBLANES, LANES)
-
-    def working(outputs, scratch, tiles):
-        state = vmem(2, outputs, 3, rows // SUBLANES, tiles, SUBLANES, LANES)
-        return [dealt_out(known, tiles), state, vmem(scratch, tiles, rows, LANES)]
-
+    dealt_out = (rows // SUBLANES, across, SUBLANES, LANES)
+    ext_own, strips_own, rates_own = pl.pallas_call(
+        functools.partial(own_kernel, steps),
+        out_shape=(
+            near(fields + 3, across, rows, LANES),
+            near(fields + 3, rows, LANES),
+            near(fields, *dealt_out),
+        ),
+        name="own_part",
+    )(*kept(own, zr_even, zr_odd))
     strips, part, part_residual = pl.pallas_call(
         functools.partial(block_kernel, times, steps, lags),
-        out_shape=(
-            near(known + 3, rows, LANES),
-            near(steps, 3, rows_lat, width),
-            near(steps, 3, rows_lat, width),
-        ),
-        scratch_shapes=[vmem(known + 3, across, rows, LANES)] + working(steps, 2 * fields, across),
+        out_shape=(near(known - fields, rows, LANES), near(steps, 3, rows_lat, width), near(steps, 3, rows_lat, width)),
+        scratch_shapes=[
+            vmem(known - fields, across, rows, LANES),
+            vmem(known - fields + 3, *dealt_out),
+            vmem(2, steps, 3, *dealt_out),
+            vmem(2 * fields, across, rows, LANES),
+        ],
         name="block_part",
-    )(*kept(own, zr_even, zr_odd, *known_of))
+    )(*kept(ext_own, rates_own, *known_of))
     updated, residual = pl.pallas_call(
         functools.partial(rim_kernel, times, steps, lags),
         out_shape=(hbm(steps, 3, rows_lat, width), hbm(steps, 3, rows_lat, width)),
         out_specs=(pl.BlockSpec(memory_space=pl.ANY),) * 2,
         scratch_shapes=[
             vmem(known + 3, 1, rows, LANES),
-            *working(1, fields, 1),
+            vmem(known, rows // SUBLANES, 1, SUBLANES, LANES),
+            vmem(2, 1, 3, rows // SUBLANES, 1, SUBLANES, LANES),
+            vmem(fields, 1, rows, LANES),
             vmem(2 * steps, 3, rows_lat, width),
             pltpu.SemaphoreType.DMA((2 * steps, 3)),
         ],
         name="rim_part",
-    )(*kept(own, strips, part, part_residual, evens, *odds))
+    )(*kept(own, strips_own, strips, part, part_residual, evens, *odds))
     return updated, residual
 
 

time: 24.4 us -> 23.9 us (0.980)
  waiting for transfers between devices: 8.2 us -> 7.64 us
    ppermute x1, waiting for transfers between devices: 2.45 us -> 0.85 us  [step(): lax.ppermute(ys, ('tm', 'gx'), with_steps('gx', odd, d))]
    ppermute x1, starting transfers between devices: 1.62 us -> 0.19 us  [step(): odds.insert(0, lax.ppermute(ys, 'gx', odd))]
    ppermute x1, starting transfers between devices: 0.16 us -> 1.59 us  [step(): lax.ppermute(ys, ('tm', 'gx'), with_steps('gx', odd, d))]
    ppermute x1, waiting for transfers between devices: 0.06 us -> 1.12 us  [step(): odds.insert(0, lax.ppermute(ys, 'gx', odd))]
    pallas_call x0 -> x1, Pallas kernels: none -> 0.34 us  [step(): pl.pallas_call(functools.partial(own_kernel, steps), out_shape=(near(fiel...]
  transfers between devices with their start and end apart: 8 -> 8, of which waited for: 5 -> 5; matrix products, arithmetic and copies ran while one was open for 0% -> 0% of each run, Pallas kernels for 15% -> 16%
where the time goes in v2:
time: 23.9 us; the launch traced here: 23.7 us
  starting transfers between devices  9.83 us (41%)
  waiting for transfers between devices  7.64 us (32%)
  Pallas kernels  5.55 us (23%)
  between operations  0.68 us (3%)
    ppermute x1, waiting for transfers between devices, step(): zr_odd = lax.ppermute(zs_odd, 'gy', pair_up('gy', True))  3.07 us
    ppermute x1, starting transfers between devices, step(): raws = [lax.ppermute(trajectory, 'tm', shifts[d]) for d in range(1, times)]  3.03 us
    ppermute x1, starting transfers between devices, step(): zr_odd = lax.ppermute(zs_odd, 'gy', pair_up('gy', True))  2.47 us
    ppermute x1, waiting for transfers between devices, step(): lax.ppermute(zr_odd[:fields], 'tm', shifts[d])  2.3 us
    pallas_call x1, Pallas kernels, step(): pl.pallas_call(functools.partial(rim_kernel, times, steps, lags), out_sha...  1.72 us
    ppermute x1, starting transfers between devices, step(): zr_even = lax.ppermute(zs_even, 'gy', pair_up('gy', False))  1.64 us
    ppermute x1, starting transfers between devices, step(): lax.ppermute(ys, ('tm', 'gx'), with_steps('gx', odd, d))  1.59 us
    pallas_call x1, Pallas kernels, step(): pl.pallas_call(functools.partial(block_kernel, times, steps, lags), out_s...  1.24 us
  transfers between devices with their start and end apart: 8, of which 5 were waited for; matrix products, arithmetic and copies ran while one was open for 0% of the time, Pallas kernels for 16%

profile of v2, /device:TPU:0, one launch (start us, length us, event | category | flops | bytes accessed | tf_op | source)
XLA Modules:
  0.0 23.7 jit_solution(13465705119279558418)
XLA Ops:
  0.6 3.0 %collective-permute-start.2 = (f32[2,3,32,256]{3,2,1,0:T(8,128)}, f32[2,3,32,256]{3,2,1,0:T(8,128)S(1)}, u32[]{:S(2)}, u32[]{:S(2)}) collective-permute-start(f32[2,3,32,256]{3,2,1,0:T(8,128)} %traj.3), channel_id=1, source_target_pairs={{0,16},{16,0},{1,17},{17,1},{2,18},{18,2},{3,19},{19,3},{4,20},{20... | collective-permute-start | bytes 589832 | tf_op jit(solution)/shard_map/ppermute | solution.py:455
  3.7 0.9 %edge_rows.1 = (f32[9,8,256]{2,1,0:T(8,128)S(1)}, f32[9,8,256]{2,1,0:T(8,128)S(1)}) custom-call(f32[2,3,32,256]{3,2,1,0:T(8,128)} %traj.3, f32[3,32,256]{2,1,0:T(8,128)} %init.3), custom_call_target="tpu_custom_call" | custom-call | tf_op jit(solution)/shard_map/edge_rows/pallas_call | solution.py:440
  4.5 1.6 %collective-permute-start = (f32[9,8,256]{2,1,0:T(8,128)S(1)}, f32[9,8,256]{2,1,0:T(8,128)S(1)}, u32[]{:S(2)}, u32[]{:S(2)}) collective-permute-start(f32[9,8,256]{2,1,0:T(8,128)S(1)} %get-tuple-element.13), channel_id=1, source_target_pairs={{0,1},{1,0},{2,3},{3,2},{4,5},{5,4},{6,7},{7,6},{8,9},{9,8},{10,11... | collective-permute-start | bytes 221192 | tf_op jit(solution)/shard_map/ppermute | solution.py:448
  6.2 2.5 %collective-permute-start.1 = (f32[9,8,256]{2,1,0:T(8,128)S(1)}, f32[9,8,256]{2,1,0:T(8,128)S(1)}, u32[]{:S(2)}, u32[]{:S(2)}) collective-permute-start(f32[9,8,256]{2,1,0:T(8,128)S(1)} %get-tuple-element.14), channel_id=1, source_target_pairs={{1,2},{2,1},{3,0},{0,3},{5,6},{6,5},{7,4},{4,7},{9,10},{10,9},{11,... | collective-permute-start | bytes 221192 | tf_op jit(solution)/shard_map/ppermute | solution.py:447
  8.7 0.3 %collective-permute-done.zr_even = f32[9,8,256]{2,1,0:T(8,128)S(1)} collective-permute-done((f32[9,8,256]{2,1,0:T(8,128)S(1)}, f32[9,8,256]{2,1,0:T(8,128)S(1)}, u32[]{:S(2)}, u32[]{:S(2)}) %collective-permute-start) | collective-permute-done | bytes 73760 | tf_op jit(solution)/shard_map/ppermute | solution.py:448
  9.0 0.3 %collective-permute-start.3 = (f32[6,8,256]{2,1,0:T(8,128)S(1)}, f32[6,8,256]{2,1,0:T(8,128)S(1)}, u32[]{:S(2)}, u32[]{:S(2)}) collective-permute-start(f32[6,8,256]{2,1,0:T(8,128)S(1)} %slice.8), channel_id=1, source_target_pairs={{0,16},{16,0},{1,17},{17,1},{2,18},{18,2},{3,19},{19,3},{4,20},{20... | collective-permute-start | bytes 147464 | tf_op jit(solution)/shard_map/ppermute | solution.py:464
  9.3 3.1 %collective-permute-done.1.zr_odd = f32[9,8,256]{2,1,0:T(8,128)S(1)} collective-permute-done((f32[9,8,256]{2,1,0:T(8,128)S(1)}, f32[9,8,256]{2,1,0:T(8,128)S(1)}, u32[]{:S(2)}, u32[]{:S(2)}) %collective-permute-start.1) | collective-permute-done | bytes 73760 | tf_op jit(solution)/shard_map/ppermute | solution.py:447
  12.3 0.5 %collective-permute-start.4 = (f32[6,8,256]{2,1,0:T(8,128)S(1)}, f32[6,8,256]{2,1,0:T(8,128)S(1)}, u32[]{:S(2)}, u32[]{:S(2)}) collective-permute-start(f32[6,8,256]{2,1,0:T(8,128)S(1)} %slice.9), channel_id=1, source_target_pairs={{0,16},{16,0},{1,17},{17,1},{2,18},{18,2},{3,19},{19,3},{4,20},{20... | collective-permute-start | bytes 147464 | tf_op jit(solution)/shard_map/ppermute | solution.py:465
  12.9 1.1 %split_block.1 = (f32[9,32,256]{2,1,0:T(8,128)S(1)}, f32[32,128]{1,0:T(8,128)S(1)}) custom-call(f32[2,3,32,256]{3,2,1,0:T(8,128)} %traj.3, f32[3,32,256]{2,1,0:T(8,128)} %init.3), custom_call_target="tpu_custom_call" | custom-call | tf_op jit(solution)/shard_map/split_block/pallas_call | solution.py:449
  14.0 0.1 pack_edges.1.refs_0_
  14.1 0.0 collective-permute-done.3.refs_1_.refs_2_
  14.1 2.3 %collective-permute-done.4.refs_2_.refs_3_ = f32[6,8,256]{2,1,0:T(8,128)S(1)} collective-permute-done((f32[6,8,256]{2,1,0:T(8,128)S(1)}, f32[6,8,256]{2,1,0:T(8,128)S(1)}, u32[]{:S(2)}, u32[]{:S(2)}) %collective-permute-start.4) | collective-permute-done | bytes 49184 | tf_op jit(solution)/shard_map/ppermute | solution.py:465
  16.4 0.0 collective-permute-done.2.refs_0_.refs_1_
  16.4 0.1 pack_others.1
  16.6 0.1 collective-permute-start.5
  16.7 1.6 %collective-permute-start.7 = (f32[48,128]{1,0:T(8,128)S(1)}, f32[48,128]{1,0:T(8,128)S(1)}, u32[]{:S(2)}, u32[]{:S(2)}) collective-permute-start(f32[48,128]{1,0:T(8,128)S(1)} %pack_edges.1.refs_0_), channel_id=1, source_target_pairs={{4,24},{8,20},{12,16},{0,28},{20,8},{24,4},{28,0},{16,12},{5,25},{... | collective-permute-start | bytes 73736 | tf_op jit(solution)/shard_map/ppermute | solution.py:466
  18.2 0.2 collective-permute-start.6
  18.4 0.3 %own_part.1 = (f32[9,2,48,128]{3,2,1,0:T(8,128)S(1)}, f32[9,48,128]{2,1,0:T(8,128)S(1)}, f32[6,6,2,8,128]{4,3,2,1,0:T(8,128)S(1)}) custom-call(f32[9,32,256]{2,1,0:T(8,128)S(1)} %get-tuple-element.12.own, f32[9,8,256]{2,1,0:T(8,128)S(1)} %collective-permute-done.zr_even, f32[9,8,256]{2,1,0:T(8,128)S(1)} %collective-permute-done.1.zr_odd), custom_call_target="tpu_custom_call" | custom-call | tf_op jit(solution)/shard_map/own_part/pallas_call | solution.py:477
  18.8 1.2 %block_part.1 = (f32[6,48,128]{2,1,0:T(8,128)S(1)}, f32[2,3,32,256]{3,2,1,0:T(8,128)S(1)}, f32[2,3,32,256]{3,2,1,0:T(8,128)S(1)}) custom-call(f32[9,2,48,128]{3,2,1,0:T(8,128)S(1)} %get-tuple-element.16.ext_own, f32[6,6,2,8,128]{4,3,2,1,0:T(8,128)S(1)} %get-tuple-element.17.rates_own, f32[2,3,32,256]{3,2,1,0:T(8,128)S(1)} %collective-permute-done.2.refs_0_.refs_1_, ...), custom_call_target="tpu_custom_call" | custom-call | tf_op jit(solution)/shard_map/block_part/pallas_call | solution.py:486
  20.0 0.8 %collective-permute-done.7.refs_0_ = f32[48,128]{1,0:T(8,128)S(1)} collective-permute-done((f32[48,128]{1,0:T(8,128)S(1)}, f32[48,128]{1,0:T(8,128)S(1)}, u32[]{:S(2)}, u32[]{:S(2)}) %collective-permute-start.7) | collective-permute-done | bytes 24608 | tf_op jit(solution)/shard_map/ppermute | solution.py:466
  20.9 1.1 %collective-permute-done.6.yr_odd = f32[48,128]{1,0:T(8,128)S(1)} collective-permute-done((f32[48,128]{1,0:T(8,128)S(1)}, f32[48,128]{1,0:T(8,128)S(1)}, u32[]{:S(2)}, u32[]{:S(2)}) %collective-permute-start.6) | collective-permute-done | bytes 24608 | tf_op jit(solution)/shard_map/ppermute | solution.py:467
  22.0 0.0 collective-permute-done.5.yr_even
  22.0 1.7 %rim_part.1 = (f32[2,3,32,256]{3,2,1,0:T(8,128)}, f32[2,3,32,256]{3,2,1,0:T(8,128)}) custom-call(f32[9,32,256]{2,1,0:T(8,128)S(1)} %get-tuple-element.12.own, f32[9,48,128]{2,1,0:T(8,128)S(1)} %get-tuple-element.15.strips_own, f32[6,48,128]{2,1,0:T(8,128)S(1)} %get-tuple-element.18.strips, f32[2,3,32,256]{3,2,1,0:T(8,128)S(1)} %get-tuple-element.19.part, ...), custom_call_target="tpu_custom_call" | custom-call | tf_op jit(solution)/shard_map/rim_part/pallas_call | solution.py:497
  (2 shorter events, 0.0 us)
Async XLA Ops:
  0.6 15.8 %collective-permute-start.2 = (f32[2,3,32,256]{3,2,1,0:T(8,128)}, f32[2,3,32,256]{3,2,1,0:T(8,128)S(1)}, u32[]{:S(2)}, u32[]{:S(2)}) collective-permute-start(f32[2,3,32,256]{3,2,1,0:T(8,128)} %traj.3), channel_id=1, source_target_pairs={{0,16},{16,0},{1,17},{17,1},{2,18},{18,2},{3,19},{19,3},{4,20},{20... | collective-permute-start | bytes 589832 | tf_op jit(solution)/shard_map/ppermute | solution.py:455
  4.5 4.4 %collective-permute-start = (f32[9,8,256]{2,1,0:T(8,128)S(1)}, f32[9,8,256]{2,1,0:T(8,128)S(1)}, u32[]{:S(2)}, u32[]{:S(2)}) collective-permute-start(f32[9,8,256]{2,1,0:T(8,128)S(1)} %get-tuple-element.13), channel_id=1, source_target_pairs={{0,1},{1,0},{2,3},{3,2},{4,5},{5,4},{6,7},{7,6},{8,9},{9,8},{10,11... | collective-permute-start | bytes 221192 | tf_op jit(solution)/shard_map/ppermute | solution.py:448
  6.2 6.2 %collective-permute-start.1 = (f32[9,8,256]{2,1,0:T(8,128)S(1)}, f32[9,8,256]{2,1,0:T(8,128)S(1)}, u32[]{:S(2)}, u32[]{:S(2)}) collective-permute-start(f32[9,8,256]{2,1,0:T(8,128)S(1)} %get-tuple-element.14), channel_id=1, source_target_pairs={{1,2},{2,1},{3,0},{0,3},{5,6},{6,5},{7,4},{4,7},{9,10},{10,9},{11,... | collective-permute-start | bytes 221192 | tf_op jit(solution)/shard_map/ppermute | solution.py:447
  9.0 5.2 %collective-permute-start.3 = (f32[6,8,256]{2,1,0:T(8,128)S(1)}, f32[6,8,256]{2,1,0:T(8,128)S(1)}, u32[]{:S(2)}, u32[]{:S(2)}) collective-permute-start(f32[6,8,256]{2,1,0:T(8,128)S(1)} %slice.8), channel_id=1, source_target_pairs={{0,16},{16,0},{1,17},{17,1},{2,18},{18,2},{3,19},{19,3},{4,20},{20... | collective-permute-start | bytes 147464 | tf_op jit(solution)/shard_map/ppermute | solution.py:464
  12.3 4.1 %collective-permute-start.4 = (f32[6,8,256]{2,1,0:T(8,128)S(1)}, f32[6,8,256]{2,1,0:T(8,128)S(1)}, u32[]{:S(2)}, u32[]{:S(2)}) collective-permute-start(f32[6,8,256]{2,1,0:T(8,128)S(1)} %slice.9), channel_id=1, source_target_pairs={{0,16},{16,0},{1,17},{17,1},{2,18},{18,2},{3,19},{19,3},{4,20},{20... | collective-permute-start | bytes 147464 | tf_op jit(solution)/shard_map/ppermute | solution.py:465
  16.6 5.4 %collective-permute-start.5 = (f32[2,48,128]{2,1,0:T(8,128)S(1)}, f32[2,48,128]{2,1,0:T(8,128)S(1)}, u32[]{:S(2)}, u32[]{:S(2)}) collective-permute-start(f32[2,48,128]{2,1,0:T(8,128)S(1)} %pack_others.1), channel_id=1, source_target_pairs={{0,4},{4,0},{8,12},{12,8},{1,5},{5,1},{9,13},{13,9},{2,6},{6,2},{1... | collective-permute-start | bytes 147464 | tf_op jit(solution)/shard_map/ppermute | solution.py:474
  16.7 4.2 %collective-permute-start.7 = (f32[48,128]{1,0:T(8,128)S(1)}, f32[48,128]{1,0:T(8,128)S(1)}, u32[]{:S(2)}, u32[]{:S(2)}) collective-permute-start(f32[48,128]{1,0:T(8,128)S(1)} %pack_edges.1.refs_0_), channel_id=1, source_target_pairs={{4,24},{8,20},{12,16},{0,28},{20,8},{24,4},{28,0},{16,12},{5,25},{... | collective-permute-start | bytes 73736 | tf_op jit(solution)/shard_map/ppermute | solution.py:466
  18.2 3.7 %collective-permute-start.6 = (f32[48,128]{1,0:T(8,128)S(1)}, f32[48,128]{1,0:T(8,128)S(1)}, u32[]{:S(2)}, u32[]{:S(2)}) collective-permute-start(f32[48,128]{1,0:T(8,128)S(1)} %pack_edges.1.refs_0_), channel_id=1, source_target_pairs={{4,8},{8,4},{12,0},{0,12},{5,9},{9,5},{13,1},{1,13},{6,10},{10,6},... | collective-permute-start | bytes 73736 | tf_op jit(solution)/shard_map/ppermute | solution.py:467

commit v3 on v2

--- a/solution.py
+++ b/solution.py
@@ -103,10 +103,9 @@
 
 def edge_kernel(steps, traj, init, zs_even, zs_odd, sems):
     rows_lat = traj.shape[-2]
-    gy_even = lax.axis_index("gy") % 2 == 0
     copies = []
-    for side, (target, south) in enumerate(((zs_even, gy_even), (zs_odd, jnp.logical_not(gy_even)))):
-        rows = pl.ds(pl.multiple_of(jnp.where(south, rows_lat - HALO, 0), SUBLANES), HALO)
+    for side, (target, south) in enumerate(((zs_even, False), (zs_odd, True))):
+        rows = pl.ds(rows_lat - HALO if south else 0, HALO)
         for l in range(steps + 1):
             source = traj.at[l, :, rows, :] if l < steps else init.at[:, rows, :]
             copies.append(pltpu.make_async_copy(source, target.at[pl.ds(3 * l, 3)], sems.at[side, l]))
@@ -127,15 +126,14 @@
 
 def other_pack_kernel(fields, *refs):
     own, others, packs = refs[0], refs[1:-1], refs[-1]
-    gy_even = lax.axis_index("gy") % 2 == 0
     packs[0] = own[...]
     for d in range(len(others) // 3):
         raw, xr_even, xr_odd = others[3 * d : 3 * d + 3]
         rows_lat, width = raw.shape[-2:]
         even = gather_columns([xr_even.at[f] for f in range(fields)], width)
         odd = gather_columns([xr_odd.at[f] for f in range(fields)], width)
-        packs[d + 1, :HALO, :] = jnp.where(gy_even, odd, even)
-        packs[d + 1, HALO + rows_lat :, :] = jnp.where(gy_even, even, odd)
+        packs[d + 1, :HALO, :] = odd
+        packs[d + 1, HALO + rows_lat :, :] = even
         for rows in range(rows_lat // SUBLANES):
             at = pl.ds(rows * SUBLANES, SUBLANES)
             tiles = [raw.at[f // 3, f % 3, at] for f in range(fields)]
@@ -144,24 +142,22 @@
 
 def pack_kernel(fields, packs, zr_even, zr_odd, ys):
     width = zr_even.shape[-1]
-    gy_even = lax.axis_index("gy") % 2 == 0
     rows_lat = packs.shape[0]
     even = gather_columns([zr_even.at[f] for f in range(fields + 3)], width)
     odd = gather_columns([zr_odd.at[f] for f in range(fields + 3)], width)
-    ys[:HALO, :] = jnp.where(gy_even, odd, even)
+    ys[:HALO, :] = odd
     ys[HALO : HALO + rows_lat, :] = packs[...]
-    ys[HALO + rows_lat :, :] = jnp.where(gy_even, even, odd)
+    ys[HALO + rows_lat :, :] = even
 
 
 def place(ext, base, own, even, odd):
     rows_lat, width = own[0].shape
-    gy_even = lax.axis_index("gy") % 2 == 0
     for f, field in enumerate(own):
         for w in range(width // LANES):
             lanes = pl.ds(w * LANES, LANES)
             ext[base + f, w, pl.ds(HALO, rows_lat), :] = field[:, lanes]
-            ext[base + f, w, pl.ds(0, HALO), :] = jnp.where(gy_even, odd[f, :, lanes], even[f, :, lanes])
-            ext[base + f, w, pl.ds(rows_lat + HALO, HALO), :] = jnp.where(gy_even, even[f, :, lanes], odd[f, :, lanes])
+            ext[base + f, w, pl.ds(0, HALO), :] = odd[f, :, lanes]
+            ext[base + f, w, pl.ds(rows_lat + HALO, HALO), :] = even[f, :, lanes]
 
 
 def within(first, count, by=0):
@@ -444,8 +440,9 @@
         scratch_shapes=[pltpu.SemaphoreType.DMA((2, steps + 1))],
         name="edge_rows",
     )(trajectory, initial)
-    zr_odd = lax.ppermute(zs_odd, "gy", pair_up("gy", True))
-    zr_even = lax.ppermute(zs_even, "gy", pair_up("gy", False))
+    count = lax.axis_size("gy")
+    zr_odd = lax.ppermute(zs_odd, "gy", [(i, (i + 1) % count) for i in range(count)])
+    zr_even = lax.ppermute(zs_even, "gy", [((i + 1) % count, i) for i in range(count)])
     own, packs = pl.pallas_call(
         functools.partial(split_kernel, fields),
         out_shape=(near(fields + 3, rows_lat, width), near(rows_lat, LANES)),

time: 23.9 us -> 25.9 us (1.084)
  waiting for transfers between devices: 7.64 us -> 9.88 us
    ppermute x2, waiting for transfers between devices: 3.37 us -> 5.61 us  [the longest x1 3.57 us: step(): lax.ppermute(zs_odd, 'gy', [(i, (i + 1) % count) for i in range(count)])]
    ppermute x2, starting transfers between devices: 4.12 us -> 3.66 us  [the longest x1 3.65 us: step(): lax.ppermute(zs_even, 'gy', [((i + 1) % count, i) for i in range(count)])]
  transfers between devices with their start and end apart: 8 -> 8, of which waited for: 5 -> 5; matrix products, arithmetic and copies ran while one was open for 0% -> 0% of each run, Pallas kernels for 16% -> 14%
where the time goes in v3:
time: 25.9 us; the launch traced here: 25.7 us
  waiting for transfers between devices  9.88 us (38%)
  starting transfers between devices  9.61 us (37%)
  Pallas kernels  5.54 us (21%)
  between operations  0.68 us (3%)
    ppermute x1, starting transfers between devices, step(): lax.ppermute(zs_even, 'gy', [((i + 1) % count, i) for i in range(count)])  3.65 us
    ppermute x1, waiting for transfers between devices, step(): lax.ppermute(zs_odd, 'gy', [(i, (i + 1) % count) for i in range(count)])  3.57 us
    ppermute x1, starting transfers between devices, step(): raws = [lax.ppermute(trajectory, 'tm', shifts[d]) for d in range(1, times)]  3.03 us
    ppermute x1, waiting for transfers between devices, step(): lax.ppermute(zr_odd[:fields], 'tm', shifts[d])  2.3 us
    ppermute x1, waiting for transfers between devices, step(): lax.ppermute(zs_even, 'gy', [((i + 1) % count, i) for i in range(count)])  2.03 us
    pallas_call x1, Pallas kernels, step(): pl.pallas_call(functools.partial(rim_kernel, times, steps, lags), out_sha...  1.72 us
    ppermute x1, starting transfers between devices, step(): lax.ppermute(ys, ('tm', 'gx'), with_steps('gx', odd, d))  1.59 us
    pallas_call x1, Pallas kernels, step(): pl.pallas_call(functools.partial(block_kernel, times, steps, lags), out_s...  1.24 us
  transfers between devices with their start and end apart: 8, of which 5 were waited for; matrix products, arithmetic and copies ran while one was open for 0% of the time, Pallas kernels for 14%

profile of v3, /device:TPU:0, one launch (start us, length us, event | category | flops | bytes accessed | tf_op | source)
XLA Modules:
  0.0 25.7 jit_solution(6740810067456925509)
XLA Ops:
  0.6 3.0 %collective-permute-start.2 = (f32[2,3,32,256]{3,2,1,0:T(8,128)}, f32[2,3,32,256]{3,2,1,0:T(8,128)S(1)}, u32[]{:S(2)}, u32[]{:S(2)}) collective-permute-start(f32[2,3,32,256]{3,2,1,0:T(8,128)} %traj.3), channel_id=1, source_target_pairs={{0,16},{16,0},{1,17},{17,1},{2,18},{18,2},{3,19},{19,3},{4,20},{20... | collective-permute-start | bytes 589832 | tf_op jit(solution)/shard_map/ppermute | solution.py:452
  3.7 0.9 %edge_rows.1 = (f32[9,8,256]{2,1,0:T(8,128)S(1)}, f32[9,8,256]{2,1,0:T(8,128)S(1)}) custom-call(f32[2,3,32,256]{3,2,1,0:T(8,128)} %traj.3, f32[3,32,256]{2,1,0:T(8,128)} %init.3), custom_call_target="tpu_custom_call" | custom-call | tf_op jit(solution)/shard_map/edge_rows/pallas_call | solution.py:436
  4.5 3.7 %collective-permute-start = (f32[9,8,256]{2,1,0:T(8,128)S(1)}, f32[9,8,256]{2,1,0:T(8,128)S(1)}, u32[]{:S(2)}, u32[]{:S(2)}) collective-permute-start(f32[9,8,256]{2,1,0:T(8,128)S(1)} %get-tuple-element.13), channel_id=1, source_target_pairs={{1,0},{2,1},{3,2},{0,3},{5,4},{6,5},{7,6},{4,7},{9,8},{10,9},{11,1... | collective-permute-start | bytes 221192 | tf_op jit(solution)/shard_map/ppermute | solution.py:445
  8.2 0.0 collective-permute-start.1
  8.2 2.0 %collective-permute-done.zr_even = f32[9,8,256]{2,1,0:T(8,128)S(1)} collective-permute-done((f32[9,8,256]{2,1,0:T(8,128)S(1)}, f32[9,8,256]{2,1,0:T(8,128)S(1)}, u32[]{:S(2)}, u32[]{:S(2)}) %collective-permute-start) | collective-permute-done | bytes 73760 | tf_op jit(solution)/shard_map/ppermute | solution.py:445
  10.2 0.5 %collective-permute-start.3 = (f32[6,8,256]{2,1,0:T(8,128)S(1)}, f32[6,8,256]{2,1,0:T(8,128)S(1)}, u32[]{:S(2)}, u32[]{:S(2)}) collective-permute-start(f32[6,8,256]{2,1,0:T(8,128)S(1)} %slice.8), channel_id=1, source_target_pairs={{0,16},{16,0},{1,17},{17,1},{2,18},{18,2},{3,19},{19,3},{4,20},{20... | collective-permute-start | bytes 147464 | tf_op jit(solution)/shard_map/ppermute | solution.py:461
  10.8 3.6 %collective-permute-done.1.zr_odd = f32[9,8,256]{2,1,0:T(8,128)S(1)} collective-permute-done((f32[9,8,256]{2,1,0:T(8,128)S(1)}, f32[9,8,256]{2,1,0:T(8,128)S(1)}, u32[]{:S(2)}, u32[]{:S(2)}) %collective-permute-start.1) | collective-permute-done | bytes 73760 | tf_op jit(solution)/shard_map/ppermute | solution.py:444
  14.4 0.5 %collective-permute-start.4 = (f32[6,8,256]{2,1,0:T(8,128)S(1)}, f32[6,8,256]{2,1,0:T(8,128)S(1)}, u32[]{:S(2)}, u32[]{:S(2)}) collective-permute-start(f32[6,8,256]{2,1,0:T(8,128)S(1)} %slice.9), channel_id=1, source_target_pairs={{0,16},{16,0},{1,17},{17,1},{2,18},{18,2},{3,19},{19,3},{4,20},{20... | collective-permute-start | bytes 147464 | tf_op jit(solution)/shard_map/ppermute | solution.py:462
  14.9 1.1 %split_block.1 = (f32[9,32,256]{2,1,0:T(8,128)S(1)}, f32[32,128]{1,0:T(8,128)S(1)}) custom-call(f32[2,3,32,256]{3,2,1,0:T(8,128)} %traj.3, f32[3,32,256]{2,1,0:T(8,128)} %init.3), custom_call_target="tpu_custom_call" | custom-call | tf_op jit(solution)/shard_map/split_block/pallas_call | solution.py:446
  16.0 0.1 pack_edges.1.refs_0_
  16.1 0.0 collective-permute-done.3.refs_1_.refs_2_
  16.1 2.3 %collective-permute-done.4.refs_2_.refs_3_ = f32[6,8,256]{2,1,0:T(8,128)S(1)} collective-permute-done((f32[6,8,256]{2,1,0:T(8,128)S(1)}, f32[6,8,256]{2,1,0:T(8,128)S(1)}, u32[]{:S(2)}, u32[]{:S(2)}) %collective-permute-start.4) | collective-permute-done | bytes 49184 | tf_op jit(solution)/shard_map/ppermute | solution.py:462
  18.4 0.0 collective-permute-done.2.refs_0_.refs_1_
  18.4 0.1 pack_others.1
  18.6 0.1 collective-permute-start.5
  18.7 1.6 %collective-permute-start.7 = (f32[48,128]{1,0:T(8,128)S(1)}, f32[48,128]{1,0:T(8,128)S(1)}, u32[]{:S(2)}, u32[]{:S(2)}) collective-permute-start(f32[48,128]{1,0:T(8,128)S(1)} %pack_edges.1.refs_0_), channel_id=1, source_target_pairs={{4,24},{8,20},{12,16},{0,28},{20,8},{24,4},{28,0},{16,12},{5,25},{... | collective-permute-start | bytes 73736 | tf_op jit(solution)/shard_map/ppermute | solution.py:463
  20.3 0.2 collective-permute-start.6
  20.5 0.3 %own_part.1 = (f32[9,2,48,128]{3,2,1,0:T(8,128)S(1)}, f32[9,48,128]{2,1,0:T(8,128)S(1)}, f32[6,6,2,8,128]{4,3,2,1,0:T(8,128)S(1)}) custom-call(f32[9,32,256]{2,1,0:T(8,128)S(1)} %get-tuple-element.12.own, f32[9,8,256]{2,1,0:T(8,128)S(1)} %collective-permute-done.zr_even, f32[9,8,256]{2,1,0:T(8,128)S(1)} %collective-permute-done.1.zr_odd), custom_call_target="tpu_custom_call" | custom-call | tf_op jit(solution)/shard_map/own_part/pallas_call | solution.py:474
  20.8 1.2 %block_part.1 = (f32[6,48,128]{2,1,0:T(8,128)S(1)}, f32[2,3,32,256]{3,2,1,0:T(8,128)S(1)}, f32[2,3,32,256]{3,2,1,0:T(8,128)S(1)}) custom-call(f32[9,2,48,128]{3,2,1,0:T(8,128)S(1)} %get-tuple-element.16.ext_own, f32[6,6,2,8,128]{4,3,2,1,0:T(8,128)S(1)} %get-tuple-element.17.rates_own, f32[2,3,32,256]{3,2,1,0:T(8,128)S(1)} %collective-permute-done.2.refs_0_.refs_1_, ...), custom_call_target="tpu_custom_call" | custom-call | tf_op jit(solution)/shard_map/block_part/pallas_call | solution.py:483
  22.0 0.8 %collective-permute-done.7.refs_0_ = f32[48,128]{1,0:T(8,128)S(1)} collective-permute-done((f32[48,128]{1,0:T(8,128)S(1)}, f32[48,128]{1,0:T(8,128)S(1)}, u32[]{:S(2)}, u32[]{:S(2)}) %collective-permute-start.7) | collective-permute-done | bytes 24608 | tf_op jit(solution)/shard_map/ppermute | solution.py:463
  22.9 1.1 %collective-permute-done.6.yr_odd = f32[48,128]{1,0:T(8,128)S(1)} collective-permute-done((f32[48,128]{1,0:T(8,128)S(1)}, f32[48,128]{1,0:T(8,128)S(1)}, u32[]{:S(2)}, u32[]{:S(2)}) %collective-permute-start.6) | collective-permute-done | bytes 24608 | tf_op jit(solution)/shard_map/ppermute | solution.py:464
  24.0 0.0 collective-permute-done.5.yr_even
  24.0 1.7 %rim_part.1 = (f32[2,3,32,256]{3,2,1,0:T(8,128)}, f32[2,3,32,256]{3,2,1,0:T(8,128)}) custom-call(f32[9,32,256]{2,1,0:T(8,128)S(1)} %get-tuple-element.12.own, f32[9,48,128]{2,1,0:T(8,128)S(1)} %get-tuple-element.15.strips_own, f32[6,48,128]{2,1,0:T(8,128)S(1)} %get-tuple-element.18.strips, f32[2,3,32,256]{3,2,1,0:T(8,128)S(1)} %get-tuple-element.19.part, ...), custom_call_target="tpu_custom_call" | custom-call | tf_op jit(solution)/shard_map/rim_part/pallas_call | solution.py:494
  (2 shorter events, 0.0 us)
Async XLA Ops:
  0.6 17.8 %collective-permute-start.2 = (f32[2,3,32,256]{3,2,1,0:T(8,128)}, f32[2,3,32,256]{3,2,1,0:T(8,128)S(1)}, u32[]{:S(2)}, u32[]{:S(2)}) collective-permute-start(f32[2,3,32,256]{3,2,1,0:T(8,128)} %traj.3), channel_id=1, source_target_pairs={{0,16},{16,0},{1,17},{17,1},{2,18},{18,2},{3,19},{19,3},{4,20},{20... | collective-permute-start | bytes 589832 | tf_op jit(solution)/shard_map/ppermute | solution.py:452
  4.5 5.7 %collective-permute-start = (f32[9,8,256]{2,1,0:T(8,128)S(1)}, f32[9,8,256]{2,1,0:T(8,128)S(1)}, u32[]{:S(2)}, u32[]{:S(2)}) collective-permute-start(f32[9,8,256]{2,1,0:T(8,128)S(1)} %get-tuple-element.13), channel_id=1, source_target_pairs={{1,0},{2,1},{3,2},{0,3},{5,4},{6,5},{7,6},{4,7},{9,8},{10,9},{11,1... | collective-permute-start | bytes 221192 | tf_op jit(solution)/shard_map/ppermute | solution.py:445
  8.2 6.2 %collective-permute-start.1 = (f32[9,8,256]{2,1,0:T(8,128)S(1)}, f32[9,8,256]{2,1,0:T(8,128)S(1)}, u32[]{:S(2)}, u32[]{:S(2)}) collective-permute-start(f32[9,8,256]{2,1,0:T(8,128)S(1)} %get-tuple-element.14), channel_id=1, source_target_pairs={{0,1},{1,2},{2,3},{3,0},{4,5},{5,6},{6,7},{7,4},{8,9},{9,10},{10,1... | collective-permute-start | bytes 221192 | tf_op jit(solution)/shard_map/ppermute | solution.py:444
  10.2 5.9 %collective-permute-start.3 = (f32[6,8,256]{2,1,0:T(8,128)S(1)}, f32[6,8,256]{2,1,0:T(8,128)S(1)}, u32[]{:S(2)}, u32[]{:S(2)}) collective-permute-start(f32[6,8,256]{2,1,0:T(8,128)S(1)} %slice.8), channel_id=1, source_target_pairs={{0,16},{16,0},{1,17},{17,1},{2,18},{18,2},{3,19},{19,3},{4,20},{20... | collective-permute-start | bytes 147464 | tf_op jit(solution)/shard_map/ppermute | solution.py:461
  14.4 4.1 %collective-permute-start.4 = (f32[6,8,256]{2,1,0:T(8,128)S(1)}, f32[6,8,256]{2,1,0:T(8,128)S(1)}, u32[]{:S(2)}, u32[]{:S(2)}) collective-permute-start(f32[6,8,256]{2,1,0:T(8,128)S(1)} %slice.9), channel_id=1, source_target_pairs={{0,16},{16,0},{1,17},{17,1},{2,18},{18,2},{3,19},{19,3},{4,20},{20... | collective-permute-start | bytes 147464 | tf_op jit(solution)/shard_map/ppermute | solution.py:462
  18.6 5.4 %collective-permute-start.5 = (f32[2,48,128]{2,1,0:T(8,128)S(1)}, f32[2,48,128]{2,1,0:T(8,128)S(1)}, u32[]{:S(2)}, u32[]{:S(2)}) collective-permute-start(f32[2,48,128]{2,1,0:T(8,128)S(1)} %pack_others.1), channel_id=1, source_target_pairs={{0,4},{4,0},{8,12},{12,8},{1,5},{5,1},{9,13},{13,9},{2,6},{6,2},{1... | collective-permute-start | bytes 147464 | tf_op jit(solution)/shard_map/ppermute | solution.py:471
  18.7 4.2 %collective-permute-start.7 = (f32[48,128]{1,0:T(8,128)S(1)}, f32[48,128]{1,0:T(8,128)S(1)}, u32[]{:S(2)}, u32[]{:S(2)}) collective-permute-start(f32[48,128]{1,0:T(8,128)S(1)} %pack_edges.1.refs_0_), channel_id=1, source_target_pairs={{4,24},{8,20},{12,16},{0,28},{20,8},{24,4},{28,0},{16,12},{5,25},{... | collective-permute-start | bytes 73736 | tf_op jit(solution)/shard_map/ppermute | solution.py:463
  20.3 3.7 %collective-permute-start.6 = (f32[48,128]{1,0:T(8,128)S(1)}, f32[48,128]{1,0:T(8,128)S(1)}, u32[]{:S(2)}, u32[]{:S(2)}) collective-permute-start(f32[48,128]{1,0:T(8,128)S(1)} %pack_edges.1.refs_0_), channel_id=1, source_target_pairs={{4,8},{8,4},{12,0},{0,12},{5,9},{9,5},{13,1},{1,13},{6,10},{10,6},... | collective-permute-start | bytes 73736 | tf_op jit(solution)/shard_map/ppermute | solution.py:464

commit v4 on v1

--- a/solution.py
+++ b/solution.py
@@ -103,10 +103,9 @@
 
 def edge_kernel(steps, traj, init, zs_even, zs_odd, sems):
     rows_lat = traj.shape[-2]
-    gy_even = lax.axis_index("gy") % 2 == 0
     copies = []
-    for side, (target, south) in enumerate(((zs_even, gy_even), (zs_odd, jnp.logical_not(gy_even)))):
-        rows = pl.ds(pl.multiple_of(jnp.where(south, rows_lat - HALO, 0), SUBLANES), HALO)
+    for side, (target, south) in enumerate(((zs_even, False), (zs_odd, True))):
+        rows = pl.ds(rows_lat - HALO if south else 0, HALO)
         for l in range(steps + 1):
             source = traj.at[l, :, rows, :] if l < steps else init.at[:, rows, :]
             copies.append(pltpu.make_async_copy(source, target.at[pl.ds(3 * l, 3)], sems.at[side, l]))
@@ -127,15 +126,14 @@
 
 def other_pack_kernel(fields, *refs):
     own, others, packs = refs[0], refs[1:-1], refs[-1]
-    gy_even = lax.axis_index("gy") % 2 == 0
     packs[0] = own[...]
     for d in range(len(others) // 3):
         raw, xr_even, xr_odd = others[3 * d : 3 * d + 3]
         rows_lat, width = raw.shape[-2:]
         even = gather_columns([xr_even.at[f] for f in range(fields)], width)
         odd = gather_columns([xr_odd.at[f] for f in range(fields)], width)
-        packs[d + 1, :HALO, :] = jnp.where(gy_even, odd, even)
-        packs[d + 1, HALO + rows_lat :, :] = jnp.where(gy_even, even, odd)
+        packs[d + 1, :HALO, :] = odd
+        packs[d + 1, HALO + rows_lat :, :] = even
         for rows in range(rows_lat // SUBLANES):
             at = pl.ds(rows * SUBLANES, SUBLANES)
             tiles = [raw.at[f // 3, f % 3, at] for f in range(fields)]
@@ -144,24 +142,22 @@
 
 def pack_kernel(fields, packs, zr_even, zr_odd, ys):
     width = zr_even.shape[-1]
-    gy_even = lax.axis_index("gy") % 2 == 0
     rows_lat = packs.shape[0]
     even = gather_columns([zr_even.at[f] for f in range(fields + 3)], width)
     odd = gather_columns([zr_odd.at[f] for f in range(fields + 3)], width)
-    ys[:HALO, :] = jnp.where(gy_even, odd, even)
+    ys[:HALO, :] = odd
     ys[HALO : HALO + rows_lat, :] = packs[...]
-    ys[HALO + rows_lat :, :] = jnp.where(gy_even, even, odd)
+    ys[HALO + rows_lat :, :] = even
 
 
 def place(ext, base, own, even, odd):
     rows_lat, width = own[0].shape
-    gy_even = lax.axis_index("gy") % 2 == 0
     for f, field in enumerate(own):
         for w in range(width // LANES):
             lanes = pl.ds(w * LANES, LANES)
             ext[base + f, w, pl.ds(HALO, rows_lat), :] = field[:, lanes]
-            ext[base + f, w, pl.ds(0, HALO), :] = jnp.where(gy_even, odd[f, :, lanes], even[f, :, lanes])
-            ext[base + f, w, pl.ds(rows_lat + HALO, HALO), :] = jnp.where(gy_even, even[f, :, lanes], odd[f, :, lanes])
+            ext[base + f, w, pl.ds(0, HALO), :] = odd[f, :, lanes]
+            ext[base + f, w, pl.ds(rows_lat + HALO, HALO), :] = even[f, :, lanes]
 
 
 def within(first, count, by=0):
@@ -400,8 +396,9 @@
         scratch_shapes=[pltpu.SemaphoreType.DMA((2, steps + 1))],
         name="edge_rows",
     )(trajectory, initial)
-    zr_odd = lax.ppermute(zs_odd, "gy", pair_up("gy", True))
-    zr_even = lax.ppermute(zs_even, "gy", pair_up("gy", False))
+    count = lax.axis_size("gy")
+    zr_odd = lax.ppermute(zs_odd, "gy", [(i, (i + 1) % count) for i in range(count)])
+    zr_even = lax.ppermute(zs_even, "gy", [((i + 1) % count, i) for i in range(count)])
     own, packs = pl.pallas_call(
         functools.partial(split_kernel, fields),
         out_shape=(near(fields + 3, rows_lat, width), near(rows_lat, LANES)),

time: 24.4 us -> 26.4 us (1.082)
  waiting for transfers between devices: 8.2 us -> 10.4 us
    ppermute x2, waiting for transfers between devices: 3.37 us -> 5.61 us  [the longest x1 3.57 us: step(): lax.ppermute(zs_odd, 'gy', [(i, (i + 1) % count) for i in range(count)])]
    ppermute x2, starting transfers between devices: 4.12 us -> 3.66 us  [the longest x1 3.65 us: step(): lax.ppermute(zs_even, 'gy', [((i + 1) % count, i) for i in range(count)])]
  transfers between devices with their start and end apart: 8 -> 8, of which waited for: 5 -> 5; matrix products, arithmetic and copies ran while one was open for 0% -> 0% of each run, Pallas kernels for 15% -> 14%
where the time goes in v4:
time: 26.4 us; the launch traced here: 26.2 us
  waiting for transfers between devices  10.4 us (39%)
  starting transfers between devices  9.61 us (36%)
  Pallas kernels  5.43 us (21%)
  between operations  0.68 us (3%)
    ppermute x1, starting transfers between devices, step(): lax.ppermute(zs_even, 'gy', [((i + 1) % count, i) for i in range(count)])  3.65 us
    ppermute x1, waiting for transfers between devices, step(): lax.ppermute(zs_odd, 'gy', [(i, (i + 1) % count) for i in range(count)])  3.57 us
    ppermute x1, starting transfers between devices, step(): raws = [lax.ppermute(trajectory, 'tm', shifts[d]) for d in range(1, times)]  3.03 us
    ppermute x1, waiting for transfers between devices, step(): lax.ppermute(ys, ('tm', 'gx'), with_steps('gx', odd, d))  2.45 us
    ppermute x1, waiting for transfers between devices, step(): lax.ppermute(zr_odd[:fields], 'tm', shifts[d])  2.31 us
    ppermute x1, waiting for transfers between devices, step(): lax.ppermute(zs_even, 'gy', [((i + 1) % count, i) for i in range(count)])  2.03 us
    pallas_call x1, Pallas kernels, step(): pl.pallas_call(functools.partial(rim_kernel, times, steps, lags), out_sha...  1.72 us
    ppermute x1, starting transfers between devices, step(): odds.insert(0, lax.ppermute(ys, 'gx', odd))  1.62 us
  transfers between devices with their start and end apart: 8, of which 5 were waited for; matrix products, arithmetic and copies ran while one was open for 0% of the time, Pallas kernels for 14%

profile of v4, /device:TPU:0, one launch (start us, length us, event | category | flops | bytes accessed | tf_op | source)
XLA Modules:
  0.0 26.2 jit_solution(5509924815379411348)
XLA Ops:
  0.6 3.0 %collective-permute-start.2 = (f32[2,3,32,256]{3,2,1,0:T(8,128)}, f32[2,3,32,256]{3,2,1,0:T(8,128)S(1)}, u32[]{:S(2)}, u32[]{:S(2)}) collective-permute-start(f32[2,3,32,256]{3,2,1,0:T(8,128)} %traj.3), channel_id=1, source_target_pairs={{0,16},{16,0},{1,17},{17,1},{2,18},{18,2},{3,19},{19,3},{4,20},{20... | collective-permute-start | bytes 589832 | tf_op jit(solution)/shard_map/ppermute | solution.py:408
  3.7 0.9 %edge_rows.1 = (f32[9,8,256]{2,1,0:T(8,128)S(1)}, f32[9,8,256]{2,1,0:T(8,128)S(1)}) custom-call(f32[2,3,32,256]{3,2,1,0:T(8,128)} %traj.3, f32[3,32,256]{2,1,0:T(8,128)} %init.3), custom_call_target="tpu_custom_call" | custom-call | tf_op jit(solution)/shard_map/edge_rows/pallas_call | solution.py:392
  4.5 3.7 %collective-permute-start = (f32[9,8,256]{2,1,0:T(8,128)S(1)}, f32[9,8,256]{2,1,0:T(8,128)S(1)}, u32[]{:S(2)}, u32[]{:S(2)}) collective-permute-start(f32[9,8,256]{2,1,0:T(8,128)S(1)} %get-tuple-element.10), channel_id=1, source_target_pairs={{1,0},{2,1},{3,2},{0,3},{5,4},{6,5},{7,6},{4,7},{9,8},{10,9},{11,1... | collective-permute-start | bytes 221192 | tf_op jit(solution)/shard_map/ppermute | solution.py:401
  8.2 0.0 collective-permute-start.1
  8.2 2.0 %collective-permute-done.zr_even = f32[9,8,256]{2,1,0:T(8,128)S(1)} collective-permute-done((f32[9,8,256]{2,1,0:T(8,128)S(1)}, f32[9,8,256]{2,1,0:T(8,128)S(1)}, u32[]{:S(2)}, u32[]{:S(2)}) %collective-permute-start) | collective-permute-done | bytes 73760 | tf_op jit(solution)/shard_map/ppermute | solution.py:401
  10.2 0.5 %collective-permute-start.3 = (f32[6,8,256]{2,1,0:T(8,128)S(1)}, f32[6,8,256]{2,1,0:T(8,128)S(1)}, u32[]{:S(2)}, u32[]{:S(2)}) collective-permute-start(f32[6,8,256]{2,1,0:T(8,128)S(1)} %slice.8), channel_id=1, source_target_pairs={{0,16},{16,0},{1,17},{17,1},{2,18},{18,2},{3,19},{19,3},{4,20},{20... | collective-permute-start | bytes 147464 | tf_op jit(solution)/shard_map/ppermute | solution.py:417
  10.8 3.6 %collective-permute-done.1.zr_odd = f32[9,8,256]{2,1,0:T(8,128)S(1)} collective-permute-done((f32[9,8,256]{2,1,0:T(8,128)S(1)}, f32[9,8,256]{2,1,0:T(8,128)S(1)}, u32[]{:S(2)}, u32[]{:S(2)}) %collective-permute-start.1) | collective-permute-done | bytes 73760 | tf_op jit(solution)/shard_map/ppermute | solution.py:400
  14.4 0.5 %collective-permute-start.4 = (f32[6,8,256]{2,1,0:T(8,128)S(1)}, f32[6,8,256]{2,1,0:T(8,128)S(1)}, u32[]{:S(2)}, u32[]{:S(2)}) collective-permute-start(f32[6,8,256]{2,1,0:T(8,128)S(1)} %slice.9), channel_id=1, source_target_pairs={{0,16},{16,0},{1,17},{17,1},{2,18},{18,2},{3,19},{19,3},{4,20},{20... | collective-permute-start | bytes 147464 | tf_op jit(solution)/shard_map/ppermute | solution.py:418
  14.9 1.1 %split_block.1 = (f32[9,32,256]{2,1,0:T(8,128)S(1)}, f32[32,128]{1,0:T(8,128)S(1)}) custom-call(f32[2,3,32,256]{3,2,1,0:T(8,128)} %traj.3, f32[3,32,256]{2,1,0:T(8,128)} %init.3), custom_call_target="tpu_custom_call" | custom-call | tf_op jit(solution)/shard_map/split_block/pallas_call | solution.py:402
  16.0 0.1 pack_edges.1.refs_0_
  16.1 0.0 collective-permute-done.3.refs_1_.refs_2_
  16.1 2.3 %collective-permute-done.4.refs_2_.refs_3_ = f32[6,8,256]{2,1,0:T(8,128)S(1)} collective-permute-done((f32[6,8,256]{2,1,0:T(8,128)S(1)}, f32[6,8,256]{2,1,0:T(8,128)S(1)}, u32[]{:S(2)}, u32[]{:S(2)}) %collective-permute-start.4) | collective-permute-done | bytes 49184 | tf_op jit(solution)/shard_map/ppermute | solution.py:418
  18.4 0.0 collective-permute-done.2.refs_0_.refs_1_
  18.4 0.1 pack_others.1
  18.6 0.1 collective-permute-start.5
  18.7 1.6 %collective-permute-start.6 = (f32[48,128]{1,0:T(8,128)S(1)}, f32[48,128]{1,0:T(8,128)S(1)}, u32[]{:S(2)}, u32[]{:S(2)}) collective-permute-start(f32[48,128]{1,0:T(8,128)S(1)} %pack_edges.1.refs_0_), channel_id=1, source_target_pairs={{4,8},{8,4},{12,0},{0,12},{5,9},{9,5},{13,1},{1,13},{6,10},{10,6},... | collective-permute-start | bytes 73736 | tf_op jit(solution)/shard_map/ppermute | solution.py:420
  20.3 0.2 collective-permute-start.7
  20.5 1.5 %block_part.1 = (f32[15,48,128]{2,1,0:T(8,128)S(1)}, f32[2,3,32,256]{3,2,1,0:T(8,128)S(1)}, f32[2,3,32,256]{3,2,1,0:T(8,128)S(1)}) custom-call(f32[9,32,256]{2,1,0:T(8,128)S(1)} %get-tuple-element.9.own, f32[9,8,256]{2,1,0:T(8,128)S(1)} %collective-permute-done.zr_even, f32[9,8,256]{2,1,0:T(8,128)S(1)} %collective-permute-done.1.zr_odd, ...), custom_call_target="tpu_custom_call" | custom-call | tf_op jit(solution)/shard_map/block_part/pallas_call | solution.py:436
  21.9 0.1 collective-permute-done.6.yr_odd
  22.0 2.5 %collective-permute-done.7.refs_0_ = f32[48,128]{1,0:T(8,128)S(1)} collective-permute-done((f32[48,128]{1,0:T(8,128)S(1)}, f32[48,128]{1,0:T(8,128)S(1)}, u32[]{:S(2)}, u32[]{:S(2)}) %collective-permute-start.7) | collective-permute-done | bytes 24608 | tf_op jit(solution)/shard_map/ppermute | solution.py:419
  24.4 0.0 collective-permute-done.5.yr_even
  24.4 1.7 %rim_part.1 = (f32[2,3,32,256]{3,2,1,0:T(8,128)}, f32[2,3,32,256]{3,2,1,0:T(8,128)}) custom-call(f32[9,32,256]{2,1,0:T(8,128)S(1)} %get-tuple-element.9.own, f32[15,48,128]{2,1,0:T(8,128)S(1)} %get-tuple-element.12.strips, f32[2,3,32,256]{3,2,1,0:T(8,128)S(1)} %get-tuple-element.13.part, f32[2,3,32,256]{3,2,1,0:T(8,128)S(1)} %get-tuple-element.14.part_residual, ...), custom_call_target="tpu_custom_call" | custom-call | tf_op jit(solution)/shard_map/rim_part/pallas_call | solution.py:446
  (2 shorter events, 0.0 us)
Async XLA Ops:
  0.6 17.8 %collective-permute-start.2 = (f32[2,3,32,256]{3,2,1,0:T(8,128)}, f32[2,3,32,256]{3,2,1,0:T(8,128)S(1)}, u32[]{:S(2)}, u32[]{:S(2)}) collective-permute-start(f32[2,3,32,256]{3,2,1,0:T(8,128)} %traj.3), channel_id=1, source_target_pairs={{0,16},{16,0},{1,17},{17,1},{2,18},{18,2},{3,19},{19,3},{4,20},{20... | collective-permute-start | bytes 589832 | tf_op jit(solution)/shard_map/ppermute | solution.py:408
  4.5 5.7 %collective-permute-start = (f32[9,8,256]{2,1,0:T(8,128)S(1)}, f32[9,8,256]{2,1,0:T(8,128)S(1)}, u32[]{:S(2)}, u32[]{:S(2)}) collective-permute-start(f32[9,8,256]{2,1,0:T(8,128)S(1)} %get-tuple-element.10), channel_id=1, source_target_pairs={{1,0},{2,1},{3,2},{0,3},{5,4},{6,5},{7,6},{4,7},{9,8},{10,9},{11,1... | collective-permute-start | bytes 221192 | tf_op jit(solution)/shard_map/ppermute | solution.py:401
  8.2 6.2 %collective-permute-start.1 = (f32[9,8,256]{2,1,0:T(8,128)S(1)}, f32[9,8,256]{2,1,0:T(8,128)S(1)}, u32[]{:S(2)}, u32[]{:S(2)}) collective-permute-start(f32[9,8,256]{2,1,0:T(8,128)S(1)} %get-tuple-element.11), channel_id=1, source_target_pairs={{0,1},{1,2},{2,3},{3,0},{4,5},{5,6},{6,7},{7,4},{8,9},{9,10},{10,1... | collective-permute-start | bytes 221192 | tf_op jit(solution)/shard_map/ppermute | solution.py:400
  10.2 5.9 %collective-permute-start.3 = (f32[6,8,256]{2,1,0:T(8,128)S(1)}, f32[6,8,256]{2,1,0:T(8,128)S(1)}, u32[]{:S(2)}, u32[]{:S(2)}) collective-permute-start(f32[6,8,256]{2,1,0:T(8,128)S(1)} %slice.8), channel_id=1, source_target_pairs={{0,16},{16,0},{1,17},{17,1},{2,18},{18,2},{3,19},{19,3},{4,20},{20... | collective-permute-start | bytes 147464 | tf_op jit(solution)/shard_map/ppermute | solution.py:417
  14.4 4.1 %collective-permute-start.4 = (f32[6,8,256]{2,1,0:T(8,128)S(1)}, f32[6,8,256]{2,1,0:T(8,128)S(1)}, u32[]{:S(2)}, u32[]{:S(2)}) collective-permute-start(f32[6,8,256]{2,1,0:T(8,128)S(1)} %slice.9), channel_id=1, source_target_pairs={{0,16},{16,0},{1,17},{17,1},{2,18},{18,2},{3,19},{19,3},{4,20},{20... | collective-permute-start | bytes 147464 | tf_op jit(solution)/shard_map/ppermute | solution.py:418
  18.6 5.9 %collective-permute-start.5 = (f32[2,48,128]{2,1,0:T(8,128)S(1)}, f32[2,48,128]{2,1,0:T(8,128)S(1)}, u32[]{:S(2)}, u32[]{:S(2)}) collective-permute-start(f32[2,48,128]{2,1,0:T(8,128)S(1)} %pack_others.1), channel_id=1, source_target_pairs={{0,4},{4,0},{8,12},{12,8},{1,5},{5,1},{9,13},{13,9},{2,6},{6,2},{1... | collective-permute-start | bytes 147464 | tf_op jit(solution)/shard_map/ppermute | solution.py:427
  18.7 3.3 %collective-permute-start.6 = (f32[48,128]{1,0:T(8,128)S(1)}, f32[48,128]{1,0:T(8,128)S(1)}, u32[]{:S(2)}, u32[]{:S(2)}) collective-permute-start(f32[48,128]{1,0:T(8,128)S(1)} %pack_edges.1.refs_0_), channel_id=1, source_target_pairs={{4,8},{8,4},{12,0},{0,12},{5,9},{9,5},{13,1},{1,13},{6,10},{10,6},... | collective-permute-start | bytes 73736 | tf_op jit(solution)/shard_map/ppermute | solution.py:420
  20.3 4.2 %collective-permute-start.7 = (f32[48,128]{1,0:T(8,128)S(1)}, f32[48,128]{1,0:T(8,128)S(1)}, u32[]{:S(2)}, u32[]{:S(2)}) collective-permute-start(f32[48,128]{1,0:T(8,128)S(1)} %pack_edges.1.refs_0_), channel_id=1, source_target_pairs={{4,24},{8,20},{12,16},{0,28},{20,8},{24,4},{28,0},{16,12},{5,25},{... | collective-permute-start | bytes 73736 | tf_op jit(solution)/shard_map/ppermute | solution.py:419
